TPU v7x, 256 devices: a whole 4x4x8 slice. The times are simulated.
256 devices in a mesh: grp: 8 (over x, core), dev: 32 (over z, y).
Axes of the slice: x: 4, y: 4, z: 8, core: 2. Of those that a mesh axis runs over, the one named last changes fastest.
Arguments:
- amplitudes: bfloat16 [256, 128, 128], P(('grp', 'dev')), may hold values from -2 to 2
- bases: bfloat16 [256, 256, 128], P(('grp', 'dev')), may hold values from -0.375 to 0.375
- factors: bfloat16 [256, 32, 256, 256], P(('grp', 'dev')), may hold values from -0.1875 to 0.1875
- intersections: bfloat16 [256, 4, 128, 128], P(('grp', 'dev')), may hold values from -0.25 to 0.25
- pair_integrals: float32 [256, 128, 128], P(('grp', 'dev')), may hold values from -6 to 6
- pno_energies: float32 [256, 128], P(('grp', 'dev')), may hold values from 0.3 to 3
- pair_shift: float32 [256], P(('grp', 'dev')), may hold values from 0.5 to 4
- pair_atoms: int32 [256, 2], P('grp'), may hold values from 0 to 31, all different within a row; in each aligned block of 32 rows (0 to 31, 32 to 63, ...) at most 3 rows name the same one
- pair_next: int32 [256, 4], P(('grp', 'dev')), may hold values from 0 to 63, as said below
Outputs:
- new_amplitudes: float32 [256, 128, 128], P(('grp', 'dev'))
Inputs may be any that keep to these rules, and one draw needn't show every extreme that they name: `pair_atoms`: each pair lists 2 different atoms of its own group. Within a group no atom is listed by more than 3 pairs, and some atom is listed by exactly 3 pairs of its group. `pair_next`: each pair lists 4 different pairs other than itself; a number below 32 is a pair of its own group, a number m from 32 on is pair m - 32 of the next group. Pairs of the last group list only pairs of their own group.
All inputs are finite; a program needn't handle non-finite values.
Results may differ from a plain program's by a relative error of at most 0.008.
Values may be sent and summed in bfloat16 or wider, within the bound.
A program may use at most 128 MiB of HBM per device.

v0:
```python
import jax
import jax.numpy as jnp
from jax import lax
from jax.sharding import PartitionSpec as P

CAP = 3
ITERS = 2


def from_behind(value, axis, steps):
    count = lax.axis_size(axis)
    first, last = (max(0, -steps), min(count, count - steps))
    return lax.ppermute(value, axis, [(source, source + steps) for source in range(first, last)])


def expand(pair_bases, pair_amps):
    halfway = jnp.einsum(
        "nai,nij->naj", pair_bases, pair_amps, preferred_element_type=jnp.float32
    ).astype(jnp.bfloat16)
    return jnp.einsum(
        "naj,nbj->nab", halfway, pair_bases, preferred_element_type=jnp.float32
    ).astype(jnp.bfloat16)


def sandwich(factor_block, expanded):
    aux_count = factor_block.shape[0]
    pao_width = factor_block.shape[1]
    flat_factor = factor_block.reshape(aux_count * pao_width, pao_width)
    squeezed = jnp.dot(flat_factor, expanded, preferred_element_type=jnp.float32).astype(
        jnp.bfloat16
    )
    squeezed = squeezed.reshape(aux_count, pao_width, pao_width)
    return jnp.einsum("kad,kbd->ab", squeezed, factor_block, preferred_element_type=jnp.float32)


def select_rows(selector, stacked):
    flat_rows = stacked.reshape(stacked.shape[0], -1)
    picked = jnp.dot(selector, flat_rows, preferred_element_type=jnp.float32).astype(jnp.bfloat16)
    return picked.reshape((selector.shape[0],) + stacked.shape[1:])


def spread_terms(selector, terms):
    return jnp.dot(
        selector.T, terms, precision=lax.Precision.HIGHEST, preferred_element_type=jnp.float32
    )


def on_device(
    amplitudes,
    bases,
    factors,
    intersections,
    pair_integrals,
    pno_energies,
    pair_shift,
    pair_atoms,
    pair_next,
):
    local_atom = lax.axis_index("dev")
    group_size = lax.axis_size("dev")
    npao = bases.shape[1]
    listed = jnp.sum((pair_atoms == local_atom).astype(jnp.int32), axis=1)
    earlier = jnp.cumsum(listed) - listed
    slot_ids = lax.iota(jnp.int32, CAP)
    selector = ((listed[None, :] == 1) & (earlier[None, :] == slot_ids[:, None])).astype(
        jnp.float32
    )
    selector_narrow = selector.astype(jnp.bfloat16)
    factor_block = factors[0]
    denominator = pno_energies[0][:, None] + pno_energies[0][None, :] + pair_shift[0]
    positions = lax.iota(jnp.int32, 2 * group_size)
    picker = (pair_next[0][:, None] == positions[None, :]).astype(jnp.bfloat16)
    pair_intersections = intersections[0]
    base_wide = bases[0].astype(jnp.float32)
    current = amplitudes
    update = None
    for iteration in range(ITERS):
        own_x = expand(bases, current)
        group_x, group_amps = (
            lax.all_gather(own_x, "dev", axis=0, tiled=True),
            lax.all_gather(current, "dev", axis=0, tiled=True),
        )
        ladder_slots = lax.map(
            lambda expanded: sandwich(factor_block, expanded), select_rows(selector_narrow, group_x)
        )
        terms = ladder_slots.reshape(CAP, npao * npao)
        arrived = lax.all_to_all(
            spread_terms(selector, terms), "dev", split_axis=0, concat_axis=0, tiled=True
        )
        summed = jnp.sum(arrived, axis=0).reshape(npao, npao)
        left_side = jnp.dot(base_wide.T, summed, precision=lax.Precision.HIGHEST)
        ladder = jnp.dot(left_side, base_wide, precision=lax.Precision.HIGHEST)
        next_amps = from_behind(group_amps, "grp", -1)
        candidates = jnp.concatenate([group_amps, next_amps], axis=0)
        neighbours = select_rows(picker, candidates)
        mixed = jnp.einsum(
            "nij,njk->nik", pair_intersections, neighbours, preferred_element_type=jnp.float32
        ).astype(jnp.bfloat16)
        coupling = jnp.einsum(
            "nik,nlk->il", mixed, pair_intersections, preferred_element_type=jnp.float32
        )
        update = -(pair_integrals[0] + ladder + coupling) / denominator
        if iteration + 1 < ITERS:
            current = update.astype(jnp.bfloat16)[None]
    return update[None]


def solution(mesh):
    return jax.shard_map(
        on_device,
        mesh=mesh,
        in_specs=(
            P(("grp", "dev"), None, None),
            P(("grp", "dev"), None, None),
            P(("grp", "dev"), None, None, None),
            P(("grp", "dev"), None, None, None),
            P(("grp", "dev"), None, None),
            P(("grp", "dev"), None),
            P(("grp", "dev")),
            P("grp", None),
            P(("grp", "dev"), None),
        ),
        out_specs=P(("grp", "dev"), None, None),
        check_vma=False,
    )
```

profile of v0, /device:TPU:4, one launch (start us, length us, event | category | flops | bytes accessed | tf_op | source)
XLA Modules:
  0.0 670.6 jit_solution(15552975760512146877)
XLA Ops:
  6.5 1.9 convolution_convert_fusion.9
  8.4 0.7 fusion.57
  9.4 7.9 %copy.17 = bf16[1,32,256,256]{2,1,3,0:T(8,128)(2,1)} copy(bf16[1,32,256,256]{3,2,1,0:T(8,128)(2,1)} %param.15) | data formatting | bytes 8388608 | tf_op args[2]
  17.4 77.3 %all-gather.10.cloned.1.call-done = bf16[8192,256]{1,0:T(8,128)(2,1)} async-done(((bf16[256,256]{1,0:T(8,128)(2,1)}), bf16[8192,256]{1,0:T(8,128)(2,1)}) %all-gather.10.cloned.1.call-update) | async-done | bytes 4194320 | tf_op jit(solution)/shard_map/all_gather | solution.py:80
  94.7 5.7 reshape.108
  100.3 2.8 convolution_convert_fusion.3
  103.3 21.1 %while.20 = (s32[]{:T(128)}, f32[3,256,256]{2,1,0:T(8,128)S(1)}, bf16[3,256,256]{2,1,0:T(8,128)(2,1)S(1)}, bf16[1,32,256,256]{3,2,1,0:T(8,128)(2,1)}, bf16[32,256,256]{1,0,2:T(8,128)(2,1)}, /*index=5*/s32[]{:T(128)}) while((s32[]{:T(128)}, f32[3,256,256]{2,1,0:T(8,128)S(1)}, bf16[3,256,256]{2,1,0:T(8,128)(2,1)S(1)}, ...), condition=%wide.region_3.4_spmd, body=%wide.region_2.3_spmd.sunk | while | flops 2149580800 | bytes 42336360 | solution.py:83
  103.3 3.5 convolution_convert_fusion.14
  106.9 1.4 copy.66
  108.3 0.8 copy-done.1
  109.0 1.3 fusion.91
  110.4 3.5 convolution_convert_fusion.14
  113.9 1.4 copy.66
  115.3 0.8 copy-done.1
  116.1 1.3 fusion.91
  117.4 3.5 convolution_convert_fusion.14
  120.9 1.4 copy.66
  122.3 0.8 copy-done.1
  123.1 1.3 fusion.91
  124.4 0.5 copy.31
  124.9 3.6 convolution_bitcast_fusion.3
  128.6 9.9 %copy.18 = f32[32,1,65536]{2,1,0:T(1,128)} copy(f32[32,1,65536]{2,0,1:T(8,128)S(1)} %convolution_bitcast_fusion.3) | data formatting | bytes 16777216 | tf_op jit(solution)/shard_map/all_to_all | solution.py:87
  138.4 5.5 all-to-all-start
  144.0 0.7 all-gather.8.cloned.1.call-update
  144.7 96.9 %all-gather.8.cloned.1.call-done = bf16[32,128,128]{2,1,0:T(8,128)(2,1)} async-done(((bf16[1,128,128]{2,1,0:T(8,128)(2,1)}), bf16[32,128,128]{2,1,0:T(8,128)(2,1)}) %all-gather.8.cloned.1.call-update) | async-done | bytes 1048592 | tf_op jit(solution)/shard_map/all_gather | solution.py:81
  241.6 1.9 collective-permute-start
  244.1 12.0 %collective-permute-done = bf16[32,128,128]{2,1,0:T(8,128)(2,1)S(1)} collective-permute-done((bf16[32,128,128]{2,1,0:T(8,128)(2,1)}, bf16[32,128,128]{2,1,0:T(8,128)(2,1)S(1)}, u32[]{:S(2)}, u32[]{:S(2)}) %collective-permute-start) | collective-permute-done | bytes 1048608 | tf_op jit(solution)/shard_map/ppermute | solution.py:13
  256.1 1.4 pad_maximum_fusion
  257.5 1.2 fusion.12
  258.8 0.5 fusion.29
  259.3 71.0 %all-to-all-done = f32[32,1,65536]{2,1,0:T(1,128)} async-done(((f32[32,1,65536]{2,1,0:T(1,128)}), f32[32,1,65536]{2,1,0:T(1,128)}, u32[]{:S(2)}, u32[]{:S(2)}) %all-to-all-start) | async-done | bytes 8388640 | tf_op jit(solution)/shard_map/all_to_all | solution.py:87
  330.2 6.5 reduce_sum.28
  336.8 0.4 fusion.49
  337.6 1.1 convolution_convert_fusion.7
  338.6 82.1 %all-gather.12.cloned.1.call-done = bf16[8192,256]{1,0:T(8,128)(2,1)} async-done(((bf16[256,256]{1,0:T(8,128)(2,1)}), bf16[8192,256]{1,0:T(8,128)(2,1)}) %all-gather.12.cloned.1.call-update) | async-done | bytes 4194320 | tf_op jit(solution)/shard_map/all_gather | solution.py:80
  420.7 5.7 reshape.114
  426.4 2.8 convolution_convert_fusion.2
  429.4 21.1 %while.21 = (s32[]{:T(128)}, f32[3,256,256]{2,1,0:T(8,128)S(1)}, bf16[3,256,256]{2,1,0:T(8,128)(2,1)S(1)}, bf16[1,32,256,256]{3,2,1,0:T(8,128)(2,1)}, bf16[32,256,256]{1,0,2:T(8,128)(2,1)}, /*index=5*/s32[]{:T(128)}) while((s32[]{:T(128)}, f32[3,256,256]{2,1,0:T(8,128)S(1)}, bf16[3,256,256]{2,1,0:T(8,128)(2,1)S(1)}, ...), condition=%wide.region_6.7_spmd, body=%wide.region_5.6_spmd.sunk | while | flops 2149580800 | bytes 42336360 | solution.py:83
  429.4 3.5 convolution_convert_fusion.15
  432.9 1.4 copy.67
  434.3 0.8 copy-done.2
  435.1 1.3 fusion.96
  436.4 3.5 convolution_convert_fusion.15
  439.9 1.4 copy.67
  441.3 0.8 copy-done.2
  442.1 1.3 fusion.96
  443.4 3.5 convolution_convert_fusion.15
  446.9 1.4 copy.67
  448.3 0.8 copy-done.2
  449.1 1.3 fusion.96
  450.4 0.5 copy.35
  451.0 3.6 convolution_bitcast_fusion.2
  454.6 9.9 %copy.21 = f32[32,1,65536]{2,1,0:T(1,128)} copy(f32[32,1,65536]{2,0,1:T(8,128)S(1)} %convolution_bitcast_fusion.2) | data formatting | bytes 16777216 | tf_op jit(solution)/shard_map/all_to_all | solution.py:87
  464.4 5.5 all-to-all-start.1
  470.0 0.5 all-gather.14.cloned.1.call-update
  470.5 96.3 %all-gather.14.cloned.1.call-done = bf16[4096,128]{1,0:T(8,128)(2,1)} async-done(((bf16[128,128]{1,0:T(8,128)(2,1)}), bf16[4096,128]{1,0:T(8,128)(2,1)}) %all-gather.14.cloned.1.call-update) | async-done | bytes 1048592 | tf_op jit(solution)/shard_map/all_gather | solution.py:81
  566.8 2.1 collective-permute-start.1
  568.9 12.4 %collective-permute-done.1 = bf16[32,128,128]{2,1,0:T(8,128)(2,1)S(1)} collective-permute-done((bf16[32,128,128]{2,1,0:T(8,128)(2,1)}, bf16[32,128,128]{2,1,0:T(8,128)(2,1)S(1)}, u32[]{:S(2)}, u32[]{:S(2)}) %collective-permute-start.1) | collective-permute-done | bytes 1048608 | tf_op jit(solution)/shard_map/ppermute | solution.py:13
  581.3 1.4 pad_maximum_fusion.1
  582.7 1.2 fusion.15
  583.9 0.5 fusion.30
  584.4 71.9 %all-to-all-done.1 = f32[32,1,65536]{2,1,0:T(1,128)} async-done(((f32[32,1,65536]{2,1,0:T(1,128)}), f32[32,1,65536]{2,1,0:T(1,128)}, u32[]{:S(2)}, u32[]{:S(2)}) %all-to-all-start.1) | async-done | bytes 8388640 | tf_op jit(solution)/shard_map/all_to_all | solution.py:87
  656.3 6.3 reduce_sum.29
  663.1 0.9 fusion.28
  (38 shorter events, 1.5 us)
Async XLA Ops:
  6.5 252.2 %copy-start = (bf16[1,4,128,128]{3,2,1,0:T(8,128)(2,1)S(1)}, bf16[1,4,128,128]{3,2,1,0:T(8,128)(2,1)}, u32[]{:S(2)}) copy-start(bf16[1,4,128,128]{3,2,1,0:T(8,128)(2,1)} %param.16) | copy-start | bytes 393220
  6.5 88.2 %all-gather.10.cloned.1.call-start = ((), (), s32[]{:S(2)}) async-start(), calls=%async_computation.3 | async-start | bytes 4325376 | tf_op jit(solution)/shard_map/all_gather | solution.py:80
  106.9 2.2 copy-start.1
  113.9 2.2 copy-start.1
  120.9 2.2 copy-start.1
  138.4 191.8 %all-to-all-start = ((f32[32,1,65536]{2,1,0:T(1,128)}), f32[32,1,65536]{2,1,0:T(1,128)}, u32[]{:S(2)}, u32[]{:S(2)}) async-start(f32[32,1,65536]{2,1,0:T(1,128)} %copy.18), calls=%async_computation | async-start | bytes 16777216 | tf_op jit(solution)/shard_map/all_to_all | solution.py:87
  143.9 113.6 %copy-start.6 = (s32[1,4]{1,0:T(1,128)S(1)}, s32[1,4]{1,0:T(1,128)}, u32[]{:S(2)}) copy-start(s32[1,4]{1,0:T(1,128)} %param.21) | copy-start | bytes 52
  143.9 97.7 %all-gather.8.cloned.1.call-start = ((), (), s32[]{:S(2)}) async-start(), calls=%async_computation.2 | async-start | bytes 1081344 | tf_op jit(solution)/shard_map/all_gather | solution.py:81
  144.7 276.1 %all-gather.12.cloned.1.call-start = ((), (), s32[]{:S(2)}) async-start(), calls=%async_computation.4 | async-start | bytes 4325376 | tf_op jit(solution)/shard_map/all_gather | solution.py:80
  241.6 14.5 %collective-permute-start = (bf16[32,128,128]{2,1,0:T(8,128)(2,1)}, bf16[32,128,128]{2,1,0:T(8,128)(2,1)S(1)}, u32[]{:S(2)}, u32[]{:S(2)}) collective-permute-start(bf16[32,128,128]{2,1,0:T(8,128)(2,1)} %all-gather.8.cloned.1.call-done), channel_id=1, source_target_pairs={{32,0},{64,32},{96,64},{128,96},{160,128},{192,160},{224,192},{33,... | collective-permute-start | bytes 3145736 | tf_op jit(solution)/shard_map/ppermute | solution.py:13
  259.2 77.6 %copy-start.3 = (bf16[1,256,128]{2,1,0:T(8,128)(2,1)S(1)}, bf16[1,256,128]{2,1,0:T(8,128)(2,1)}, u32[]{:S(2)}) copy-start(bf16[1,256,128]{2,1,0:T(8,128)(2,1)} %param.14) | copy-start | bytes 196612
  259.2 78.0 %copy-start.5 = (f32[1,128,128]{2,1,0:T(8,128)S(1)}, f32[1,128,128]{2,1,0:T(8,128)}, u32[]{:S(2)}) copy-start(f32[1,128,128]{2,1,0:T(8,128)} %param.17) | copy-start | bytes 196612
  259.2 78.0 %copy-start.7 = (f32[1,128]{1,0:T(1,128)S(1)}, f32[1,128]{1,0:T(1,128)}, u32[]{:S(2)}) copy-start(f32[1,128]{1,0:T(1,128)} %param.18) | copy-start | bytes 1540
  337.5 88.8 %copy-start.4 = (bf16[128,128]{1,0:T(8,128)(2,1)}, bf16[128,128]{1,0:T(8,128)(2,1)S(1)}, u32[]{:S(2)}) copy-start(bf16[128,128]{1,0:T(8,128)(2,1)S(1)} %fusion.31) | copy-start | bytes 98308
  432.9 2.2 copy-start.2
  439.9 2.2 copy-start.2
  446.9 2.2 copy-start.2
  464.4 191.9 %all-to-all-start.1 = ((f32[32,1,65536]{2,1,0:T(1,128)}), f32[32,1,65536]{2,1,0:T(1,128)}, u32[]{:S(2)}, u32[]{:S(2)}) async-start(f32[32,1,65536]{2,1,0:T(1,128)} %copy.21), calls=%async_computation.1 | async-start | bytes 16777216 | tf_op jit(solution)/shard_map/all_to_all | solution.py:87
  469.9 96.8 %all-gather.14.cloned.1.call-start = ((), (), s32[]{:S(2)}) async-start(), calls=%async_computation.5 | async-start | bytes 1081344 | tf_op jit(solution)/shard_map/all_gather | solution.py:81
  566.8 14.5 %collective-permute-start.1 = (bf16[32,128,128]{2,1,0:T(8,128)(2,1)}, bf16[32,128,128]{2,1,0:T(8,128)(2,1)S(1)}, u32[]{:S(2)}, u32[]{:S(2)}) collective-permute-start(bf16[32,128,128]{2,1,0:T(8,128)(2,1)} %bitcast.189), channel_id=1, source_target_pairs={{32,0},{64,32},{96,64},{128,96},{160,128},{192,160},{224,192},{33,... | collective-permute-start | bytes 3145736 | tf_op jit(solution)/shard_map/ppermute | solution.py:13
Sparse Core Ops, SparseCore 0:
  9.9 84.7 all-gather.9
  147.3 94.2 all-gather.7
  338.8 81.9 all-gather.11
  473.0 93.7 all-gather.13
where the time goes:
time: 675 us; the launch traced here: 671 us
  waiting for transfers between devices  521 us (77%)
  local copies, waits for them, and re-layouts  53.6 us (8%)
  matrix products  50 us (7%)
  other arithmetic  16.6 us (2%)
  starting transfers between devices  15.1 us (2%)
  between operations  14 us (2%)
    all_gather x2, waiting for transfers between devices, on_device(): lax.all_gather(current, 'dev', axis=0, tiled=True)  193 us
    all_gather x2, waiting for transfers between devices, on_device(): lax.all_gather(own_x, 'dev', axis=0, tiled=True)  159 us
    all_to_all x2, waiting for transfers between devices, on_device(): lax.all_to_all(spread_terms(selector, terms), 'dev', split_axis=0, concat...  143 us
    ppermute x2, waiting for transfers between devices, from_behind(): lax.ppermute(value, axis, [(source, source + steps) for source in range(f...  24.4 us
    dot_general x6, matrix products, sandwich(): jnp.dot(flat_factor, expanded, preferred_element_type=jnp.float32)  21 us
    all_to_all x2, local copies, waits for them, and re-layouts, on_device(): lax.all_to_all(spread_terms(selector, terms), 'dev', split_axis=0, concat...  19.7 us
  transfers between devices with their start and end apart: 8, of which 8 were waited for; matrix products, arithmetic and copies ran while one was open for 2% of the time, Pallas kernels for 0%

commit v1 on v0

v1 whole, which is shorter than its diff:
```python
import jax
import jax.numpy as jnp
from jax import lax
from jax.sharding import PartitionSpec as P

CAP = 3
ITERS = 2


def from_behind(value, axis, steps):
    count = lax.axis_size(axis)
    first, last = (max(0, -steps), min(count, count - steps))
    return lax.ppermute(value, axis, [(source, source + steps) for source in range(first, last)])


def select_rows(selector, stacked):
    flat_rows = stacked.reshape(stacked.shape[0], -1)
    picked = jnp.dot(selector, flat_rows, preferred_element_type=jnp.float32).astype(jnp.bfloat16)
    return picked.reshape((selector.shape[0],) + stacked.shape[1:])


def on_device(
    amplitudes,
    bases,
    factors,
    intersections,
    pair_integrals,
    pno_energies,
    pair_shift,
    pair_atoms,
    pair_next,
):
    local_atom = lax.axis_index("dev")
    group_size = lax.axis_size("dev")
    listed = jnp.sum((pair_atoms == local_atom).astype(jnp.int32), axis=1)
    earlier = jnp.cumsum(listed) - listed
    slot_ids = lax.iota(jnp.int32, CAP)
    selector = ((listed[None, :] == 1) & (earlier[None, :] == slot_ids[:, None])).astype(
        jnp.bfloat16
    )
    factor_block = factors[0]
    denominator = pno_energies[0][:, None] + pno_energies[0][None, :] + pair_shift[0]
    positions = lax.iota(jnp.int32, 2 * group_size)
    picker = (pair_next[0][:, None] == positions[None, :]).astype(jnp.bfloat16)
    pair_intersections = intersections[0]
    slot_bases = select_rows(selector, lax.all_gather(bases, "dev", axis=0, tiled=True))
    half = jnp.einsum(
        "sai,kad->ksid", slot_bases, factor_block, preferred_element_type=jnp.float32
    ).astype(jnp.bfloat16)
    inner = jnp.einsum(
        "ksid,sdj->skij", half, slot_bases, preferred_element_type=jnp.float32
    ).astype(jnp.bfloat16)
    current = amplitudes
    update = None
    for iteration in range(ITERS):
        group_amps = lax.all_gather(current, "dev", axis=0, tiled=True)
        slot_amps = select_rows(selector, group_amps)
        left = jnp.einsum(
            "skij,sjl->skil", inner, slot_amps, preferred_element_type=jnp.float32
        ).astype(jnp.bfloat16)
        terms = jnp.einsum(
            "skil,skml->sim", left, inner, preferred_element_type=jnp.float32
        ).astype(jnp.bfloat16)
        spread = select_rows(selector.T, terms)
        arrived = lax.all_to_all(spread, "dev", split_axis=0, concat_axis=0, tiled=True)
        ladder = jnp.sum(arrived.astype(jnp.float32), axis=0)
        next_amps = from_behind(group_amps, "grp", -1)
        candidates = jnp.concatenate([group_amps, next_amps], axis=0)
        neighbours = select_rows(picker, candidates)
        mixed = jnp.einsum(
            "nij,njk->nik", pair_intersections, neighbours, preferred_element_type=jnp.float32
        ).astype(jnp.bfloat16)
        coupling = jnp.einsum(
            "nik,nlk->il", mixed, pair_intersections, preferred_element_type=jnp.float32
        )
        update = -(pair_integrals[0] + ladder + coupling) / denominator
        if iteration + 1 < ITERS:
            current = update.astype(jnp.bfloat16)[None]
    return update[None]


def solution(mesh):
    return jax.shard_map(
        on_device,
        mesh=mesh,
        in_specs=(
            P(("grp", "dev"), None, None),
            P(("grp", "dev"), None, None),
            P(("grp", "dev"), None, None, None),
            P(("grp", "dev"), None, None, None),
            P(("grp", "dev"), None, None),
            P(("grp", "dev"), None),
            P(("grp", "dev")),
            P("grp", None),
            P(("grp", "dev"), None),
        ),
        out_specs=P(("grp", "dev"), None, None),
        check_vma=False,
    )
```

time: 675 us -> 332 us (0.49)
  waiting for transfers between devices: 521 us -> 269 us
  local copies, waits for them, and re-layouts: 53.6 us -> 4.92 us
  matrix products: 50 us -> 23.4 us
  other arithmetic: 16.6 us -> 4.01 us
    all_to_all x2, waiting for transfers between devices: 143 us -> 13.9 us  [on_device(): lax.all_to_all(spread, 'dev', split_axis=0, concat_axis=0, tiled=True)]
    all_gather x4 -> x3, waiting for transfers between devices: 353 us -> 229 us  [the longest x2 154 us: on_device(): group_amps = lax.all_gather(current, 'dev', axis=0, tiled=True)]
    dot_general x20 -> x3, matrix products: 40.9 us -> 10.1 us  [the longest x1 5.65 us: on_device(): jnp.einsum('ksid,sdj->skij', half, slot_bases, preferred_element_type=jnp...]
    all_to_all x2 -> x0, local copies, waits for them, and re-layouts: 19.7 us -> none  [on_device(): lax.all_to_all(spread_terms(selector, terms), 'dev', split_axis=0, concat...]
    while x18 -> x0, local copies, waits for them, and re-layouts: 13 us -> none
    reduce_sum x2, other arithmetic: 12.9 us -> 1.53 us  [on_device(): ladder = jnp.sum(arrived.astype(jnp.float32), axis=0)]
    reshape x2 -> x1, local copies, waits for them, and re-layouts: 11.3 us -> 2.29 us  [select_rows(): flat_rows = stacked.reshape(stacked.shape[0], -1)]
  transfers between devices with their start and end apart: 8 -> 7, of which waited for: 8 -> 7; matrix products, arithmetic and copies ran while one was open for 2% -> 2% of each run, Pallas kernels for 0% -> 0%
where the time goes in v1:
time: 332 us; the launch traced here: 331 us
  waiting for transfers between devices  269 us (81%)
  matrix products  23.4 us (7%)
  starting transfers between devices  16.1 us (5%)
  between operations  13.9 us (4%)
  local copies, waits for them, and re-layouts  4.92 us (1%)
  other arithmetic  4.01 us (1%)
    all_gather x2, waiting for transfers between devices, on_device(): group_amps = lax.all_gather(current, 'dev', axis=0, tiled=True)  154 us
    all_gather x1, waiting for transfers between devices, on_device(): lax.all_gather(bases, 'dev', axis=0, tiled=True)  75.6 us
    ppermute x2, waiting for transfers between devices, from_behind(): lax.ppermute(value, axis, [(source, source + steps) for source in range(f...  24.1 us
    all_to_all x2, waiting for transfers between devices, on_device(): lax.all_to_all(spread, 'dev', split_axis=0, concat_axis=0, tiled=True)  13.9 us
    all_to_all x2, starting transfers between devices, on_device(): lax.all_to_all(spread, 'dev', split_axis=0, concat_axis=0, tiled=True)  11.8 us
    dot_general x7, matrix products, select_rows(): jnp.dot(selector, flat_rows, preferred_element_type=jnp.float32)  10.3 us
  transfers between devices with their start and end apart: 7, of which 7 were waited for; matrix products, arithmetic and copies ran while one was open for 2% of the time, Pallas kernels for 0%

profile of v1, /device:TPU:4, one launch (start us, length us, event | category | flops | bytes accessed | tf_op | source)
XLA Modules:
  0.0 331.2 jit_solution(18424834743950528445)
XLA Ops:
  6.5 0.0 copy-start
  6.5 0.0 all-gather.7.cloned.1.call-start
  6.5 0.7 all-gather.7.cloned.1.call-update
  7.3 0.0 all-gather.5.cloned.1.call-start
  7.3 0.7 all-gather.5.cloned.1.call-update
  8.0 0.7 fusion.96
  8.7 0.1 copy.12
  8.8 0.1 reduce-window.8
  8.9 0.1 reduce
  9.0 80.3 %all-gather.7.cloned.1.call-done = bf16[32,128,128]{2,1,0:T(8,128)(2,1)} async-done(((bf16[1,128,128]{2,1,0:T(8,128)(2,1)}), bf16[32,128,128]{2,1,0:T(8,128)(2,1)}) %all-gather.7.cloned.1.call-update) | async-done | bytes 1048592 | tf_op jit(solution)/shard_map/all_gather | solution.py:56
  89.3 2.5 fusion.51
  91.9 75.6 %all-gather.5.cloned.1.call-done = bf16[32,256,128]{2,1,0:T(8,128)(2,1)} async-done(((bf16[1,256,128]{2,1,0:T(8,128)(2,1)}), bf16[32,256,128]{2,1,0:T(8,128)(2,1)}) %all-gather.5.cloned.1.call-update) | async-done | bytes 2097168 | tf_op jit(solution)/shard_map/all_gather | solution.py:46
  167.5 2.9 fusion.28
  170.4 5.6 %fusion.15 = bf16[3,32,128,128]{3,2,1,0:T(8,128)(2,1)S(1)} fusion(bf16[1,32,256,256]{3,2,1,0:T(8,128)(2,1)} %param.11, bf16[1,3,256,128]{3,1,2,0:T(4,128)(2,1)S(1)} %fusion.28), kind=kOutput, calls=%fused_computation.18 | convolution fusion | flops 2420637696 | bytes 7536640 | tf_op jit(solution)/shard_map/ksid,sdj->skij/dot_general | solution.py:50
  176.0 2.7 fusion.55
  178.7 0.5 fusion.26
  179.2 1.3 copy.36
  180.5 0.0 copy-start.2
  180.5 5.8 %all-to-all-start = ((bf16[32,128,128]{2,1,0:T(8,128)(2,1)}), bf16[32,128,128]{2,1,0:T(8,128)(2,1)}, u32[]{:S(2)}, u32[]{:S(2)}) async-start(bf16[32,128,128]{2,1,0:T(8,128)(2,1)} %bitcast.204), calls=%async_computation | async-start | bytes 2097152 | tf_op jit(solution)/shard_map/all_to_all | solution.py:65
  186.3 0.0 all-gather.9.cloned.1.call-start
  186.4 2.1 collective-permute-start
  189.1 0.0 copy-start.4
  189.2 11.8 %collective-permute-done = bf16[32,128,128]{2,1,0:T(8,128)(2,1)S(1)} collective-permute-done((bf16[32,128,128]{2,1,0:T(8,128)(2,1)}, bf16[32,128,128]{2,1,0:T(8,128)(2,1)S(1)}, u32[]{:S(2)}, u32[]{:S(2)}) %collective-permute-start) | collective-permute-done | bytes 1048608 | tf_op jit(solution)/shard_map/ppermute | solution.py:13
  200.9 1.4 pad_maximum_fusion
  202.3 0.0 copy-done.2
  202.3 1.2 fusion.43
  203.6 6.3 %all-to-all-done = bf16[32,128,128]{2,1,0:T(8,128)(2,1)} async-done(((bf16[32,128,128]{2,1,0:T(8,128)(2,1)}), bf16[32,128,128]{2,1,0:T(8,128)(2,1)}, u32[]{:S(2)}, u32[]{:S(2)}) %all-to-all-start) | async-done | bytes 1048608 | tf_op jit(solution)/shard_map/all_to_all | solution.py:65
  209.9 1.4 convert_reduce_fusion.1
  211.3 0.0 copy-done
  211.3 0.0 copy-done.4
  211.3 1.9 fusion.70
  213.2 0.0 all-gather.9.cloned.1.call-update
  213.2 73.5 %all-gather.9.cloned.1.call-done = bf16[4096,128]{1,0:T(8,128)(2,1)} async-done(((bf16[128,128]{1,0:T(8,128)(2,1)}), bf16[4096,128]{1,0:T(8,128)(2,1)}) %all-gather.9.cloned.1.call-update) | async-done | bytes 1048592 | tf_op jit(solution)/shard_map/all_gather | solution.py:56
  286.8 2.3 reshape.87
  289.1 1.5 fusion.52
  290.5 1.8 fusion.58
  292.3 0.0 copy-start.1
  292.3 0.5 fusion.27
  292.8 1.3 copy.41
  294.1 6.0 %all-to-all-start.1 = ((bf16[32,128,128]{2,1,0:T(8,128)(2,1)}), bf16[32,128,128]{2,1,0:T(8,128)(2,1)S(1)}, u32[]{:S(2)}, u32[]{:S(2)}) async-start(bf16[32,128,128]{2,1,0:T(8,128)(2,1)} %bitcast.54), calls=%async_computation.1 | async-start | bytes 2097152 | tf_op jit(solution)/shard_map/all_to_all | solution.py:65
  300.1 0.0 copy-done.1
  300.1 0.0 copy-start.3
  300.1 2.1 collective-permute-start.1
  302.2 12.3 %collective-permute-done.1 = bf16[32,128,128]{2,1,0:T(8,128)(2,1)S(1)} collective-permute-done((bf16[32,128,128]{2,1,0:T(8,128)(2,1)S(1)}, bf16[32,128,128]{2,1,0:T(8,128)(2,1)S(1)}, u32[]{:S(2)}, u32[]{:S(2)}) %collective-permute-start.1) | collective-permute-done | bytes 1048608 | tf_op jit(solution)/shard_map/ppermute | solution.py:13
  314.5 0.2 pad_maximum_fusion.1
  314.7 1.2 fusion.46
  315.9 7.6 %all-to-all-done.1 = bf16[32,128,128]{2,1,0:T(8,128)(2,1)S(1)} async-done(((bf16[32,128,128]{2,1,0:T(8,128)(2,1)}), bf16[32,128,128]{2,1,0:T(8,128)(2,1)S(1)}, u32[]{:S(2)}, u32[]{:S(2)}) %all-to-all-start.1) | async-done | bytes 1048608 | tf_op jit(solution)/shard_map/all_to_all | solution.py:65
  323.5 0.2 convert_reduce_fusion
  323.6 0.0 copy-done.3
  323.6 1.1 fusion.69
  (3 shorter events, 0.0 us)
Async XLA Ops:
  6.5 204.7 %copy-start = (bf16[1,4,128,128]{3,2,1,0:T(8,128)(2,1)S(1)}, bf16[1,4,128,128]{3,2,1,0:T(8,128)(2,1)}, u32[]{:S(2)}) copy-start(bf16[1,4,128,128]{3,2,1,0:T(8,128)(2,1)} %param.12) | copy-start | bytes 393220
  6.5 82.8 %all-gather.7.cloned.1.call-start = ((), (), s32[]{:S(2)}) async-start(), calls=%async_computation.3 | async-start | bytes 1081344 | tf_op jit(solution)/shard_map/all_gather | solution.py:56
  7.3 160.3 %all-gather.5.cloned.1.call-start = ((), (), s32[]{:S(2)}) async-start(), calls=%async_computation.2 | async-start | bytes 2162688 | tf_op jit(solution)/shard_map/all_gather | solution.py:46
  180.5 21.9 %copy-start.2 = (s32[1,4]{1,0:T(1,128)S(1)}, s32[1,4]{1,0:T(1,128)}, u32[]{:S(2)}) copy-start(s32[1,4]{1,0:T(1,128)} %param.17) | copy-start | bytes 52
  180.5 29.4 %all-to-all-start = ((bf16[32,128,128]{2,1,0:T(8,128)(2,1)}), bf16[32,128,128]{2,1,0:T(8,128)(2,1)}, u32[]{:S(2)}, u32[]{:S(2)}) async-start(bf16[32,128,128]{2,1,0:T(8,128)(2,1)} %bitcast.204), calls=%async_computation | async-start | bytes 2097152 | tf_op jit(solution)/shard_map/all_to_all | solution.py:65
  186.3 100.4 %all-gather.9.cloned.1.call-start = ((), (), s32[]{:S(2)}) async-start(), calls=%async_computation.4 | async-start | bytes 1081344 | tf_op jit(solution)/shard_map/all_gather | solution.py:56
  186.4 14.5 %collective-permute-start = (bf16[32,128,128]{2,1,0:T(8,128)(2,1)}, bf16[32,128,128]{2,1,0:T(8,128)(2,1)S(1)}, u32[]{:S(2)}, u32[]{:S(2)}) collective-permute-start(bf16[32,128,128]{2,1,0:T(8,128)(2,1)} %all-gather.7.cloned.1.call-done), channel_id=1, source_target_pairs={{32,0},{64,32},{96,64},{128,96},{160,128},{192,160},{224,192},{33,... | collective-permute-start | bytes 3145736 | tf_op jit(solution)/shard_map/ppermute | solution.py:13
  189.1 22.1 %copy-start.4 = (f32[1,128]{1,0:T(1,128)S(1)}, f32[1,128]{1,0:T(1,128)}, u32[]{:S(2)}) copy-start(f32[1,128]{1,0:T(1,128)} %param.14) | copy-start | bytes 1540
  292.3 7.8 %copy-start.1 = (bf16[4096,128]{1,0:T(8,128)(2,1)S(1)}, bf16[4096,128]{1,0:T(8,128)(2,1)}, u32[]{:S(2)}) copy-start(bf16[4096,128]{1,0:T(8,128)(2,1)} %all-gather.9.cloned.1.call-done) | copy-start | bytes 3145732
  294.1 29.4 %all-to-all-start.1 = ((bf16[32,128,128]{2,1,0:T(8,128)(2,1)}), bf16[32,128,128]{2,1,0:T(8,128)(2,1)S(1)}, u32[]{:S(2)}, u32[]{:S(2)}) async-start(bf16[32,128,128]{2,1,0:T(8,128)(2,1)} %bitcast.54), calls=%async_computation.1 | async-start | bytes 2097152 | tf_op jit(solution)/shard_map/all_to_all | solution.py:65
  300.1 23.5 %copy-start.3 = (f32[1,128,128]{2,1,0:T(8,128)S(1)}, f32[1,128,128]{2,1,0:T(8,128)}, u32[]{:S(2)}) copy-start(f32[1,128,128]{2,1,0:T(8,128)} %param.13) | copy-start | bytes 196612
  300.1 14.4 %collective-permute-start.1 = (bf16[32,128,128]{2,1,0:T(8,128)(2,1)S(1)}, bf16[32,128,128]{2,1,0:T(8,128)(2,1)S(1)}, u32[]{:S(2)}, u32[]{:S(2)}) collective-permute-start(bf16[32,128,128]{2,1,0:T(8,128)(2,1)S(1)} %bitcast.206), channel_id=1, source_target_pairs={{32,0},{64,32},{96,64},{128,96},{160,128},{192,160},{224,192},{33,... | collective-permute-start | bytes 3145736 | tf_op jit(solution)/shard_map/ppermute | solution.py:13
Sparse Core Ops, SparseCore 0:
  9.9 79.3 all-gather.6
  91.9 75.5 all-gather.4
  213.3 73.3 all-gather.8

commit v2 on v1

v2 whole, which is shorter than its diff:
```python
import jax
import jax.numpy as jnp
from jax import lax
from jax.experimental import pallas as pl
from jax.experimental.pallas import tpu as pltpu
from jax.sharding import PartitionSpec as P

CAP = 3
ITERS = 2
NZ = 8
NY = 4
NOV = 4
F32 = jnp.float32
BF16 = jnp.bfloat16
MESH = pl.DeviceIdType.MESH
Z_ORDER = (4, 3, 5, 2, 6, 1, 7)
NT = (((1,), (1,)), ((), ()))
SELK, JSEL, RET, JN = 0, 12, 15, 31


def tables(pair_atoms, pair_next, z, y):
    pairs = lax.iota(jnp.int32, NZ * NY)
    same = jnp.any(pair_atoms[:, :, None, None] == pair_atoms[None, None, :, :], axis=3)
    rank = jnp.sum((same & (pairs[None, None, :] < pairs[:, None, None])).astype(jnp.int32), axis=2)
    steps = lax.iota(jnp.int32, NY)
    row_atoms = z * NY + (y + steps) % NY
    slots = lax.iota(jnp.int32, CAP)
    match = (pair_atoms[None, None] == row_atoms[:, None, None, None]) & (
        rank[None, None] == slots[None, :, None, None]
    )
    slot_pair = jnp.sum(jnp.where(match, pairs[None, None, :, None], 0), axis=(2, 3))
    selk = (z - slot_pair // NY + NZ) % NZ
    jsel = (y - slot_pair[0] % NY + NY) % NY
    code = jnp.where(
        pair_atoms // NY == z, ((y - pair_atoms % NY + NY) % NY) * CAP + rank, -1
    )
    targets = ((z + lax.iota(jnp.int32, NZ)) % NZ) * NY + y
    ret = jnp.sum(
        jnp.where(targets[:, None, None] == pairs[None, :, None], code[None], 0), axis=1
    )
    listed = pair_next[0]
    jn = (y - listed % NY + NY) % NY
    idx = (listed // (NZ * NY)) * NZ + (z - (listed % (NZ * NY)) // NY + NZ) % NZ
    tab = jnp.concatenate([selk.reshape(-1), jsel, ret.reshape(-1), jn])
    tile = jnp.pad(idx[None], ((0, 7), (0, 128 - NOV)))
    return tab, tile


def kernel(
    tab, shift, nxt, energy, b_h, c_h, f_h, s_h, i_h,
    out,
    f_v, s_v, i_v, z_b, z_c0, z_c1, n_c0, n_c1, yb_o, y_b, yc_o, y_c0, y_c1, yn_o, y_n0, y_n1, n_in, n_s,
    b_t, g_v, cc, p_v, y_t0, y_t1, bk, z_t, den, base,
    loc, zb_s, zb_r, zc_s, zc_r, nx_s, nx_r, yb_s, yb_r, yc_s, yc_r,
    fw_s, fw_r, yn_s, yn_r, yt_s, yt_r, zt_s, zt_r,
):
    z_c, n_c, y_c, y_n, y_t = (z_c0, z_c1), (n_c0, n_c1), (y_c0, y_c1), (y_n0, y_n1), (y_t0, y_t1)
    g = lax.axis_index("grp")
    d = lax.axis_index("dev")
    z, y = d // NY, d % NY
    groups = lax.axis_size("grp")
    npno = c_h.shape[1]
    kaux = f_h.shape[0]

    def at_z(k):
        return {"grp": g, "dev": ((z + k) % NZ) * NY + y}

    def at_y(j):
        return {"grp": g, "dev": z * NY + (y + j) % NY}

    before = {"grp": (g + groups - 1) % groups, "dev": d}
    after = {"grp": (g + 1) % groups, "dev": d}

    sent = []

    def send(src, dst, ss, rs, where):
        copy = pltpu.make_async_remote_copy(
            src_ref=src, dst_ref=dst, send_sem=ss, recv_sem=rs,
            device_id=where, device_id_type=MESH,
        )
        copy.start()
        sent.append(copy)
        return copy

    own = [
        pltpu.make_async_copy(f_h, f_v, loc.at[0]),
        pltpu.make_async_copy(b_h, z_b.at[0], loc.at[1]),
        pltpu.make_async_copy(c_h, z_c[0].at[0], loc.at[2]),
        pltpu.make_async_copy(s_h, s_v, loc.at[3]),
        pltpu.make_async_copy(i_h, i_v, loc.at[4]),
    ]
    for copy in own[1:]:
        copy.start()
    own[0].start()

    barrier = pltpu.get_barrier_semaphore()
    partners = [at_z(k) for k in Z_ORDER] + [at_y(j) for j in range(1, NY)] + [before, after]
    for partner in partners:
        pl.semaphore_signal(barrier, inc=1, device_id=partner, device_id_type=MESH)
    cc[...] = jnp.zeros_like(cc)
    wide = jnp.broadcast_to(energy[...], (npno, npno))
    den[...] = wide + wide.T + shift[0]
    pl.semaphore_wait(barrier, len(partners))

    zb = [send(b_h, z_b.at[k], zb_s.at[k - 1], zb_r.at[k - 1], at_z(k)) for k in Z_ORDER]
    zc = [
        send(c_h, z_c[0].at[k], zc_s.at[0, k - 1], zc_r.at[0, k - 1], at_z(k)) for k in Z_ORDER
    ]
    nx = [
        send(nxt, n_in.at[j - 1], nx_s.at[j - 1], nx_r.at[j - 1], at_y(j)) for j in range(1, NY)
    ]
    for copy in nx:
        copy.wait_recv()
    to_s = pltpu.make_async_copy(n_in, n_s, loc.at[5])
    to_s.start()
    to_s.wait()

    own[1].wait()
    for copy in zb:
        copy.wait_recv()
    yb = []
    for s in range(CAP):
        for j in range(1, NY):
            yb_o[j - 1, s] = z_b[tab[SELK + j * CAP + s]]
        for j in range(1, NY):
            yb.append(
                send(yb_o.at[j - 1, s], y_b.at[j, s], yb_s.at[j - 1, s], yb_r.at[j - 1, s], at_y(j))
            )
        y_b[0, s] = z_b[tab[SELK + s]]

    def share_amps(it, zc):
        for copy in zc:
            copy.wait_recv()
        yc = []
        for j in range(1, NY):
            for s in range(CAP):
                yc_o[it, j - 1, s] = z_c[it][tab[SELK + j * CAP + s]]
            yc.append(
                send(yc_o.at[it, j - 1], y_c[it].at[j], yc_s.at[it, j - 1], yc_r.at[it, j - 1], at_y(j))
            )
        for s in range(CAP):
            y_c[it][0, s] = z_c[it][tab[SELK + s]]
        fw = send(
            z_c[it], n_c[it].at[pl.ds(NZ, NZ)], fw_s.at[it], fw_r.at[it], before
        )
        n_c[it][:NZ] = z_c[it][...]
        return yc, fw

    def share_neighbours(it, fw):
        fw.wait_recv()
        yn = []
        for j in range(1, NY):
            for n in range(NOV):
                yn_o[it, j - 1, n] = n_c[it][n_s[NY - 1 - j, 0, n]]
            yn.append(
                send(yn_o.at[it, j - 1], y_n[it].at[j], yn_s.at[it, j - 1], yn_r.at[it, j - 1], at_y(j))
            )
        return yn

    def my_neighbour(it, n):
        return y_n[it][tab[JN + n], n]

    own[2].wait()
    yc, fw = share_amps(0, zc)
    yn = share_neighbours(0, fw)

    own[0].wait()
    for copy in yb:
        copy.wait_recv()
    for s in range(CAP):
        b_t[pl.ds(s * npno, npno), :] = y_b[tab[JSEL + s], s].T
    slot_bases = [y_b[tab[JSEL + s], s] for s in range(CAP)]

    def project(k, carry):
        half = jnp.dot(b_t[...], f_v[k], preferred_element_type=F32).astype(BF16)
        column = pl.multiple_of(k * npno, npno)
        for s in range(CAP):
            g_v[s, :, pl.ds(column, npno)] = jnp.dot(
                half[s * npno:(s + 1) * npno], slot_bases[s], preferred_element_type=F32
            ).astype(BF16)
        return carry

    lax.fori_loop(0, kaux, project, 0)
    own[3].wait()
    own[4].wait()

    for it in range(ITERS):
        for copy in yc:
            copy.wait_recv()
        yt = []
        for s in range(CAP):
            amps = y_c[it][tab[JSEL + s], s]
            cc[s, :npno, :npno] = amps
            cc[s, npno:, npno:] = amps
            for h in range(kaux // 2):
                span = pl.ds(h * 2 * npno, 2 * npno)
                p_v[s, :, span] = jnp.dot(
                    g_v[s, :, span], cc[s], preferred_element_type=F32
                ).astype(BF16)
            term = lax.dot_general(p_v[s], g_v[s], NT, preferred_element_type=F32)
            y_t[it][s] = term.astype(BF16)
            for j in range(1, NY):
                yt.append(
                    send(
                        y_t[it].at[s], y_t[it].at[j * CAP + s],
                        yt_s.at[it, j - 1, s], yt_r.at[it, j - 1, s], at_y(j),
                    )
                )
        if it > 0:
            yn = share_neighbours(it, fw)
        for copy in yt:
            copy.wait_recv()
        zt = []
        for k in (0,) + Z_ORDER:
            first, second = tab[RET + 2 * k], tab[RET + 2 * k + 1]
            total = y_t[it][jnp.maximum(first, 0)].astype(F32) * (first >= 0).astype(F32)
            total += y_t[it][jnp.maximum(second, 0)].astype(F32) * (second >= 0).astype(F32)
            if k == 0:
                base[...] = i_v[...] + total
            else:
                bk[it, k] = total.astype(BF16)
                zt.append(
                    send(bk.at[it, k], z_t.at[it, k], zt_s.at[it, k - 1], zt_r.at[it, k - 1], at_z(k))
                )
        for n in range(NOV):
            y_n[it][0, n] = n_c[it][tab[JN + NOV + n]]
        for copy in yn:
            copy.wait_recv()
        coupling = base[...]
        for n in range(NOV):
            mixed = jnp.dot(s_v[n], my_neighbour(it, n), preferred_element_type=F32).astype(BF16)
            coupling += lax.dot_general(mixed, s_v[n], NT, preferred_element_type=F32)
        base[...] = coupling
        for copy in zt:
            copy.wait_recv()
        total = base[...]
        for k in range(1, NZ):
            total += z_t[it, k].astype(F32)
        if it + 1 < ITERS:
            z_c[it + 1][0] = (-total / den[...]).astype(BF16)
            zc = [
                send(
                    z_c[it + 1].at[0], z_c[it + 1].at[k],
                    zc_s.at[it + 1, k - 1], zc_r.at[it + 1, k - 1], at_z(k),
                )
                for k in Z_ORDER
            ]
            yc, fw = share_amps(it + 1, zc)
        else:
            out[...] = total
    for copy in sent:
        copy.wait_send()


def on_device(
    amplitudes,
    bases,
    factors,
    intersections,
    pair_integrals,
    pno_energies,
    pair_shift,
    pair_atoms,
    pair_next,
):
    d = lax.axis_index("dev")
    z, y = d // NY, d % NY
    tab, tile = tables(pair_atoms, pair_next, z, y)
    tab = jnp.concatenate([tab, tile[0, :NOV]])
    npno, npao, kaux = amplitudes.shape[1], bases.shape[1], factors.shape[1]
    vm = pltpu.VMEM
    dma = pltpu.SemaphoreType.DMA
    smem = pl.BlockSpec(memory_space=pltpu.SMEM)
    vmem = pl.BlockSpec(memory_space=pltpu.VMEM)
    hbm = pl.BlockSpec(memory_space=pl.ANY)
    total = pl.pallas_call(
        kernel,
        out_shape=jax.ShapeDtypeStruct((npno, npno), F32),
        in_specs=[smem, smem, vmem, vmem, hbm, hbm, hbm, hbm, hbm],
        out_specs=vmem,
        scratch_shapes=[
            vm((kaux, npao, npao), BF16),
            vm((NOV, npno, npno), BF16),
            vm((npno, npno), F32),
            vm((NZ, npao, npno), BF16),
            vm((NZ, npno, npno), BF16),
            vm((NZ, npno, npno), BF16),
            vm((2 * NZ, npno, npno), BF16),
            vm((2 * NZ, npno, npno), BF16),
            vm((NY - 1, CAP, npao, npno), BF16),
            vm((NY, CAP, npao, npno), BF16),
            vm((ITERS, NY - 1, CAP, npno, npno), BF16),
            vm((NY, CAP, npno, npno), BF16),
            vm((NY, CAP, npno, npno), BF16),
            vm((ITERS, NY - 1, NOV, npno, npno), BF16),
            vm((NY, NOV, npno, npno), BF16),
            vm((NY, NOV, npno, npno), BF16),
            vm((NY - 1, 8, 128), jnp.int32),
            pltpu.SMEM((NY - 1, 8, 128), jnp.int32),
            vm((CAP * npno, npao), BF16),
            vm((CAP, npno, kaux * npno), BF16),
            vm((CAP, 2 * npno, 2 * npno), BF16),
            vm((CAP, npno, kaux * npno), BF16),
            vm((NY * CAP, npno, npno), BF16),
            vm((NY * CAP, npno, npno), BF16),
            vm((ITERS, NZ, npno, npno), BF16),
            vm((ITERS, NZ, npno, npno), BF16),
            vm((npno, npno), F32),
            vm((npno, npno), F32),
            dma((6,)),
            dma((NZ - 1,)),
            dma((NZ - 1,)),
            dma((ITERS, NZ - 1)),
            dma((ITERS, NZ - 1)),
            dma((NY - 1,)),
            dma((NY - 1,)),
            dma((NY - 1, CAP)),
            dma((NY - 1, CAP)),
            dma((ITERS, NY - 1)),
            dma((ITERS, NY - 1)),
            dma((ITERS,)),
            dma((ITERS,)),
            dma((ITERS, NY - 1)),
            dma((ITERS, NY - 1)),
            dma((ITERS, NY - 1, CAP)),
            dma((ITERS, NY - 1, CAP)),
            dma((ITERS, NZ - 1)),
            dma((ITERS, NZ - 1)),
        ],
        compiler_params=pltpu.CompilerParams(
            collective_id=0, has_side_effects=True, vmem_limit_bytes=48 << 20
        ),
        name="ladder",
    )(
        tab, pair_shift, tile, pno_energies, bases[0], amplitudes[0], factors[0],
        intersections[0], pair_integrals[0],
    )
    denominator = pno_energies[0][:, None] + pno_energies[0][None, :] + pair_shift[0]
    return (-total / denominator)[None]


def solution(mesh):
    return jax.shard_map(
        on_device,
        mesh=mesh,
        in_specs=(
            P(("grp", "dev"), None, None),
            P(("grp", "dev"), None, None),
            P(("grp", "dev"), None, None, None),
            P(("grp", "dev"), None, None, None),
            P(("grp", "dev"), None, None),
            P(("grp", "dev"), None),
            P(("grp", "dev")),
            P("grp", None),
            P(("grp", "dev"), None),
        ),
        out_specs=P(("grp", "dev"), None, None),
        check_vma=False,
    )
```

time: 332 us -> 104 us (0.31)
  waiting for transfers between devices: 269 us -> 0 us
  Pallas kernels: 0 us -> 90.4 us
  matrix products: 23.4 us -> 0 us
  starting transfers between devices: 16.1 us -> 0 us
  between operations: 13.9 us -> 0.7 us
    all_gather x3 -> x0, waiting for transfers between devices: 229 us -> none  [the longest x2 154 us: on_device(): group_amps = lax.all_gather(current, 'dev', axis=0, tiled=True)]
    pallas_call x0 -> x1, Pallas kernels: none -> 90.4 us  [on_device(): pl.pallas_call(kernel, out_shape=jax.ShapeDtypeStruct((npno, npno), F32),...]
    ppermute x2 -> x0, waiting for transfers between devices: 24.1 us -> none  [from_behind(): lax.ppermute(value, axis, [(source, source + steps) for source in range(f...]
    dot_general x12 -> x0, matrix products: 23.4 us -> none  [the longest x7 10.3 us: select_rows(): jnp.dot(selector, flat_rows, preferred_element_type=jnp.float32)]
    all_to_all x2 -> x0, waiting for transfers between devices: 13.9 us -> none  [on_device(): lax.all_to_all(spread, 'dev', split_axis=0, concat_axis=0, tiled=True)]
    all_to_all x2 -> x0, starting transfers between devices: 11.8 us -> none  [on_device(): lax.all_to_all(spread, 'dev', split_axis=0, concat_axis=0, tiled=True)]
    ppermute x2 -> x0, starting transfers between devices: 4.15 us -> none  [from_behind(): lax.ppermute(value, axis, [(source, source + steps) for source in range(f...]
    unnamed x12, local copies, waits for them, and re-layouts: 2.54 us -> 6.19 us
  transfers between devices with their start and end apart: 7 -> 0, of which waited for: 7 -> 0; matrix products, arithmetic and copies ran while one was open for 2% -> 0% of each run, Pallas kernels for 0% -> 0%
where the time goes in v2:
time: 104 us; the launch traced here: 103 us
  Pallas kernels  90.4 us (87%)
  local copies, waits for them, and re-layouts  6.73 us (6%)
  other arithmetic  4.94 us (5%)
    pallas_call x1, Pallas kernels, on_device(): pl.pallas_call(kernel, out_shape=jax.ShapeDtypeStruct((npno, npno), F32),...  90.4 us
    unnamed x12, local copies, waits for them, and re-layouts  6.19 us

profile of v2, /device:TPU:4, one launch (start us, length us, event | category | flops | bytes accessed | tf_op | source)
XLA Modules:
  0.0 102.7 jit_solution(14636870138096905989)
XLA Ops:
  0.7 0.7 fusion.5
  1.4 0.1 iota_compare_fusion.1
  1.4 0.7 fusion.4
  2.1 0.8 broadcast_compare_fusion
  2.9 0.8 compare_reduce_fusion
  3.7 0.1 convert_reduce_fusion
  3.8 0.7 compare_select_fusion.18
  4.5 0.1 select_reduce_fusion.1
  4.7 0.2 select_reduce_fusion
  4.8 0.1 slice_reduce_fusion
  5.0 0.1 copy.22
  5.1 0.1 reduce_sum.31
  5.2 0.1 copy.23
  5.3 0.1 reshape.97
  5.4 0.1 concatenate.3.tab
  5.4 0.0 copy-start
  5.4 2.2 %copy-done = bf16[1,32,256,256]{3,2,1,0:T(8,128)(2,1)S(1)} copy-done((bf16[1,32,256,256]{3,2,1,0:T(8,128)(2,1)S(1)}, bf16[1,32,256,256]{3,2,1,0:T(8,128)(2,1)}, u32[]{:S(2)}) %copy-start) | copy-done | bytes 4194328
  7.6 0.0 copy-start.1
  7.6 0.9 copy-done.1
  8.5 0.0 copy-start.2
  8.5 0.8 copy-done.2
  9.4 0.0 copy-start.3
  9.4 0.8 copy-done.3
  10.2 0.0 copy-start.4
  10.2 0.8 copy-done.4
  11.0 0.0 copy-start.5
  11.0 0.7 copy-done.5
  11.6 90.4 %ladder.1 = f32[128,128]{1,0:T(8,128)S(1)} custom-call(s32[39]{0:T(128)S(1)} %concatenate.3.tab, f32[1]{0:T(128)} %copy.24.shift, s32[8,128]{1,0:T(8,128)S(1)} %pad.4.nxt, f32[1,128]{1,0:T(1,128)S(1)} %copy-done.5, bf16[256,128]{1,0:T(8,128)(2,1)S(1)} %bitcast.32, bf16[128,128]{1,0:T(8,128)(2,1)S(1)} %bitcast.34, bf16[32,256,256]{2,1,0:T(8,128)(2,1)S(1)} %bitcast.30, ...), custom_call_target="tpu_custom_call" | custom-call | tf_op jit(solution)/shard_map/ladder/pallas_call | solution.py:276
  102.0 0.7 divide_bitcast_fusion
  (6 shorter events, 0.1 us)
Async XLA Ops:
  5.4 2.2 %copy-start = (bf16[1,32,256,256]{3,2,1,0:T(8,128)(2,1)S(1)}, bf16[1,32,256,256]{3,2,1,0:T(8,128)(2,1)}, u32[]{:S(2)}) copy-start(bf16[1,32,256,256]{3,2,1,0:T(8,128)(2,1)} %param.11) | copy-start | bytes 12582916
  7.6 0.9 copy-start.1
  8.5 0.8 copy-start.2
  9.4 0.8 copy-start.3
  10.2 0.8 copy-start.4
  11.0 0.7 copy-start.5

commit v3 on v2

--- a/solution.py
+++ b/solution.py
@@ -10,47 +10,54 @@
 NZ = 8
 NY = 4
 NOV = 4
+BATCH = 4
 F32 = jnp.float32
 BF16 = jnp.bfloat16
 MESH = pl.DeviceIdType.MESH
 Z_ORDER = (4, 3, 5, 2, 6, 1, 7)
 NT = (((1,), (1,)), ((), ()))
-SELK, JSEL, RET, JN = 0, 12, 15, 31
-
-
-def tables(pair_atoms, pair_next, z, y):
-    pairs = lax.iota(jnp.int32, NZ * NY)
-    same = jnp.any(pair_atoms[:, :, None, None] == pair_atoms[None, None, :, :], axis=3)
-    rank = jnp.sum((same & (pairs[None, None, :] < pairs[:, None, None])).astype(jnp.int32), axis=2)
-    steps = lax.iota(jnp.int32, NY)
-    row_atoms = z * NY + (y + steps) % NY
-    slots = lax.iota(jnp.int32, CAP)
-    match = (pair_atoms[None, None] == row_atoms[:, None, None, None]) & (
-        rank[None, None] == slots[None, :, None, None]
-    )
-    slot_pair = jnp.sum(jnp.where(match, pairs[None, None, :, None], 0), axis=(2, 3))
-    selk = (z - slot_pair // NY + NZ) % NZ
-    jsel = (y - slot_pair[0] % NY + NY) % NY
-    code = jnp.where(
-        pair_atoms // NY == z, ((y - pair_atoms % NY + NY) % NY) * CAP + rank, -1
-    )
-    targets = ((z + lax.iota(jnp.int32, NZ)) % NZ) * NY + y
-    ret = jnp.sum(
-        jnp.where(targets[:, None, None] == pairs[None, :, None], code[None], 0), axis=1
-    )
-    listed = pair_next[0]
-    jn = (y - listed % NY + NY) % NY
-    idx = (listed // (NZ * NY)) * NZ + (z - (listed % (NZ * NY)) // NY + NZ) % NZ
-    tab = jnp.concatenate([selk.reshape(-1), jsel, ret.reshape(-1), jn])
-    tile = jnp.pad(idx[None], ((0, 7), (0, 128 - NOV)))
-    return tab, tile
+PAIR, SELK, JSEL, RET, TAB = 0, 12, 24, 27, 43
+
+
+def scan_pairs(pa_s, tab, z, y):
+    def visit(p, carry):
+        counts, found = carry
+        counts, found = list(counts), list(found)
+        for j in range(NY):
+            atom = z * NY + ((y + j) & (NY - 1))
+            hit = (pa_s[0, p] == atom) | (pa_s[1, p] == atom)
+            for s in range(CAP):
+                found[j * CAP + s] = jnp.where(
+                    hit & (counts[j] == s), p, found[j * CAP + s]
+                )
+            counts[j] = counts[j] + hit.astype(jnp.int32)
+        return tuple(counts), tuple(found)
+
+    zero, none = jnp.int32(0), jnp.int32(-1)
+    _, found = lax.fori_loop(0, NZ * NY, visit, ((zero,) * NY, (none,) * (NY * CAP)))
+    for i in range(NY * CAP):
+        pair = jnp.maximum(found[i], 0)
+        tab[PAIR + i] = found[i]
+        tab[SELK + i] = (z - (pair >> 2)) & (NZ - 1)
+        if i < CAP:
+            tab[JSEL + i] = (y - (pair & (NY - 1))) & (NY - 1)
+    for k in range(NZ):
+        pair = ((z + k) & (NZ - 1)) * NY + y
+        for i in range(2):
+            atom = pa_s[i, pair]
+            j = (y - (atom & (NY - 1))) & (NY - 1)
+            mate = ((NY - j) & (NY - 1)) * CAP
+            rank = jnp.where(tab[PAIR + mate + 1] == pair, 1, 0) + jnp.where(
+                tab[PAIR + mate + 2] == pair, 2, 0
+            )
+            tab[RET + 2 * k + i] = jnp.where((atom >> 2) == z, j * CAP + rank, -1)
 
 
 def kernel(
-    tab, shift, nxt, energy, b_h, c_h, f_h, s_h, i_h,
+    pa_h, pn_h, sh_h, e_h, b_h, c_h, f_h, s_h, i_h,
     out,
-    f_v, s_v, i_v, z_b, z_c0, z_c1, n_c0, n_c1, yb_o, y_b, yc_o, y_c0, y_c1, yn_o, y_n0, y_n1, n_in, n_s,
-    b_t, g_v, cc, p_v, y_t0, y_t1, bk, z_t, den, base,
+    pa_s, pn_s, sh_s, e_v, tab, f_v, s_v, i_v, z_b, z_c0, z_c1, n_c0, n_c1, yb_o, y_b, yc_o, y_c0, y_c1, yn_o, y_n0, y_n1, n_in, n_s,
+    b_t, y_s, g_v, cc, p_v, y_t0, y_t1, bk, z_t, den, base,
     loc, zb_s, zb_r, zc_s, zc_r, nx_s, nx_r, yb_s, yb_r, yc_s, yc_r,
     fw_s, fw_r, yn_s, yn_r, yt_s, yt_r, zt_s, zt_r,
 ):
@@ -89,6 +96,14 @@
         pltpu.make_async_copy(s_h, s_v, loc.at[3]),
         pltpu.make_async_copy(i_h, i_v, loc.at[4]),
     ]
+    small = [
+        pltpu.make_async_copy(pa_h, pa_s, loc.at[6]),
+        pltpu.make_async_copy(pn_h, pn_s, loc.at[7]),
+        pltpu.make_async_copy(sh_h, sh_s, loc.at[8]),
+        pltpu.make_async_copy(e_h, e_v, loc.at[9]),
+    ]
+    for copy in small:
+        copy.start()
     for copy in own[1:]:
         copy.start()
     own[0].start()
@@ -98,8 +113,9 @@
     for partner in partners:
         pl.semaphore_signal(barrier, inc=1, device_id=partner, device_id_type=MESH)
     cc[...] = jnp.zeros_like(cc)
-    wide = jnp.broadcast_to(energy[...], (npno, npno))
-    den[...] = wide + wide.T + shift[0]
+    for copy in small:
+        copy.wait()
+    scan_pairs(pa_s, tab, z, y)
     pl.semaphore_wait(barrier, len(partners))
 
     zb = [send(b_h, z_b.at[k], zb_s.at[k - 1], zb_r.at[k - 1], at_z(k)) for k in Z_ORDER]
@@ -107,7 +123,7 @@
         send(c_h, z_c[0].at[k], zc_s.at[0, k - 1], zc_r.at[0, k - 1], at_z(k)) for k in Z_ORDER
     ]
     nx = [
-        send(nxt, n_in.at[j - 1], nx_s.at[j - 1], nx_r.at[j - 1], at_y(j)) for j in range(1, NY)
+        send(pn_h, n_in.at[j - 1], nx_s.at[j - 1], nx_r.at[j - 1], at_y(j)) for j in range(1, NY)
     ]
     for copy in nx:
         copy.wait_recv()
@@ -115,6 +131,8 @@
     to_s.start()
     to_s.wait()
 
+    wide = jnp.broadcast_to(e_v[...], (npno, npno))
+    den[...] = wide + wide.T + sh_s[0]
     own[1].wait()
     for copy in zb:
         copy.wait_recv()
@@ -151,14 +169,15 @@
         yn = []
         for j in range(1, NY):
             for n in range(NOV):
-                yn_o[it, j - 1, n] = n_c[it][n_s[NY - 1 - j, 0, n]]
+                listed = n_s[NY - 1 - j, 0, n]
+                yn_o[it, j - 1, n] = n_c[it][(listed >> 5) * NZ + ((z - ((listed & 31) >> 2)) & (NZ - 1))]
             yn.append(
                 send(yn_o.at[it, j - 1], y_n[it].at[j], yn_s.at[it, j - 1], yn_r.at[it, j - 1], at_y(j))
             )
         return yn
 
     def my_neighbour(it, n):
-        return y_n[it][tab[JN + n], n]
+        return y_n[it][(y - (pn_s[0, n] & (NY - 1))) & (NY - 1), n]
 
     own[2].wait()
     yc, fw = share_amps(0, zc)
@@ -169,18 +188,21 @@
         copy.wait_recv()
     for s in range(CAP):
         b_t[pl.ds(s * npno, npno), :] = y_b[tab[JSEL + s], s].T
-    slot_bases = [y_b[tab[JSEL + s], s] for s in range(CAP)]
-
-    def project(k, carry):
-        half = jnp.dot(b_t[...], f_v[k], preferred_element_type=F32).astype(BF16)
-        column = pl.multiple_of(k * npno, npno)
+    def project(kk, carry):
+        for u in range(BATCH):
+            half = jnp.dot(b_t[...], f_v[kk * BATCH + u], preferred_element_type=F32).astype(BF16)
+            for s in range(CAP):
+                y_s[s, u * npno:(u + 1) * npno] = half[s * npno:(s + 1) * npno]
+        column = pl.multiple_of(kk * (npno * BATCH), npno * BATCH)
         for s in range(CAP):
-            g_v[s, :, pl.ds(column, npno)] = jnp.dot(
-                half[s * npno:(s + 1) * npno], slot_bases[s], preferred_element_type=F32
+            inner = jnp.dot(
+                y_s[s], y_b[tab[JSEL + s], s], preferred_element_type=F32
             ).astype(BF16)
+            for u in range(BATCH):
+                g_v[s, :, pl.ds(column + u * npno, npno)] = inner[u * npno:(u + 1) * npno]
         return carry
 
-    lax.fori_loop(0, kaux, project, 0)
+    lax.fori_loop(0, kaux // BATCH, project, 0)
     own[3].wait()
     own[4].wait()
 
@@ -223,7 +245,8 @@
                     send(bk.at[it, k], z_t.at[it, k], zt_s.at[it, k - 1], zt_r.at[it, k - 1], at_z(k))
                 )
         for n in range(NOV):
-            y_n[it][0, n] = n_c[it][tab[JN + NOV + n]]
+            listed = pn_s[0, n]
+            y_n[it][0, n] = n_c[it][(listed >> 5) * NZ + ((z - ((listed & 31) >> 2)) & (NZ - 1))]
         for copy in yn:
             copy.wait_recv()
         coupling = base[...]
@@ -263,22 +286,22 @@
     pair_atoms,
     pair_next,
 ):
-    d = lax.axis_index("dev")
-    z, y = d // NY, d % NY
-    tab, tile = tables(pair_atoms, pair_next, z, y)
-    tab = jnp.concatenate([tab, tile[0, :NOV]])
     npno, npao, kaux = amplitudes.shape[1], bases.shape[1], factors.shape[1]
     vm = pltpu.VMEM
     dma = pltpu.SemaphoreType.DMA
-    smem = pl.BlockSpec(memory_space=pltpu.SMEM)
     vmem = pl.BlockSpec(memory_space=pltpu.VMEM)
     hbm = pl.BlockSpec(memory_space=pl.ANY)
     total = pl.pallas_call(
         kernel,
         out_shape=jax.ShapeDtypeStruct((npno, npno), F32),
-        in_specs=[smem, smem, vmem, vmem, hbm, hbm, hbm, hbm, hbm],
+        in_specs=[hbm] * 9,
         out_specs=vmem,
         scratch_shapes=[
+            pltpu.SMEM(pair_atoms.shape[::-1], jnp.int32),
+            pltpu.SMEM(pair_next.shape, jnp.int32),
+            pltpu.SMEM((1,), F32),
+            vm((1, npno), F32),
+            pltpu.SMEM((TAB,), jnp.int32),
             vm((kaux, npao, npao), BF16),
             vm((NOV, npno, npno), BF16),
             vm((npno, npno), F32),
@@ -295,9 +318,10 @@
             vm((ITERS, NY - 1, NOV, npno, npno), BF16),
             vm((NY, NOV, npno, npno), BF16),
             vm((NY, NOV, npno, npno), BF16),
-            vm((NY - 1, 8, 128), jnp.int32),
-            pltpu.SMEM((NY - 1, 8, 128), jnp.int32),
+            vm((NY - 1, 1, NOV), jnp.int32),
+            pltpu.SMEM((NY - 1, 1, NOV), jnp.int32),
             vm((CAP * npno, npao), BF16),
+            vm((CAP, BATCH * npno, npao), BF16),
             vm((CAP, npno, kaux * npno), BF16),
             vm((CAP, 2 * npno, 2 * npno), BF16),
             vm((CAP, npno, kaux * npno), BF16),
@@ -307,7 +331,7 @@
             vm((ITERS, NZ, npno, npno), BF16),
             vm((npno, npno), F32),
             vm((npno, npno), F32),
-            dma((6,)),
+            dma((10,)),
             dma((NZ - 1,)),
             dma((NZ - 1,)),
             dma((ITERS, NZ - 1)),
@@ -328,11 +352,11 @@
             dma((ITERS, NZ - 1)),
         ],
         compiler_params=pltpu.CompilerParams(
-            collective_id=0, has_side_effects=True, vmem_limit_bytes=48 << 20
+            collective_id=0, has_side_effects=True, vmem_limit_bytes=67043328
         ),
         name="ladder",
     )(
-        tab, pair_shift, tile, pno_energies, bases[0], amplitudes[0], factors[0],
+        pair_atoms.T, pair_next, pair_shift, pno_energies, bases[0], amplitudes[0], factors[0],
         intersections[0], pair_integrals[0],
     )
     denominator = pno_energies[0][:, None] + pno_energies[0][None, :] + pair_shift[0]

time: 104 us -> 88.2 us (0.85)
  local copies, waits for them, and re-layouts: 6.73 us -> 0 us
  Pallas kernels: 90.4 us -> 85.1 us
  other arithmetic: 4.94 us -> 1.58 us
    unnamed x12 -> x0, local copies, waits for them, and re-layouts: 6.19 us -> none
    pallas_call x1, Pallas kernels: 90.4 us -> 85.1 us  [on_device(): pl.pallas_call(kernel, out_shape=jax.ShapeDtypeStruct((npno, npno), F32),...]
    add x3 -> x0, other arithmetic: 1.38 us -> none  [the longest x2 1.37 us: tables(): idx = listed // (NZ * NY) * NZ + (z - listed % (NZ * NY) // NY + NZ) % NZ]
where the time goes in v3:
time: 88.2 us; the launch traced here: 87.3 us
  Pallas kernels  85.1 us (96%)
  other arithmetic  1.58 us (2%)
    pallas_call x1, Pallas kernels, on_device(): pl.pallas_call(kernel, out_shape=jax.ShapeDtypeStruct((npno, npno), F32),...  85.1 us

profile of v3, /device:TPU:4, one launch (start us, length us, event | category | flops | bytes accessed | tf_op | source)
XLA Modules:
  0.0 87.3 jit_solution(16024429741447094828)
XLA Ops:
  0.7 85.1 %ladder.1 = f32[128,128]{1,0:T(8,128)} custom-call(s32[2,32]{1,0:T(2,128)} %bitcast.17, s32[1,4]{1,0:T(1,128)} %pn_h.1, f32[1]{0:T(128)} %copy.10.sh_h, f32[1,128]{1,0:T(1,128)} %e_h.1, bf16[256,128]{1,0:T(8,128)(2,1)} %bitcast.13, bf16[128,128]{1,0:T(8,128)(2,1)} %bitcast.15, bf16[32,256,256]{2,1,0:T(8,128)(2,1)} %bitcast.11, ...), custom_call_target="tpu_custom_call" | custom-call | tf_op jit(solution)/shard_map/ladder/pallas_call | solution.py:294
  85.7 1.6 %divide_bitcast_fusion = f32[1,128,128]{2,1,0:T(8,128)} fusion(f32[128,128]{1,0:T(8,128)} %ladder.1, f32[]{:T(128)} %bitcast.10, f32[128]{0:T(128)} %bitcast.16), kind=kLoop, calls=%fused_computation | loop fusion | flops 65536 | bytes 131588 | tf_op jit(solution)/shard_map/broadcast_in_dim | solution.py:363

commit v4 on v1

v4 whole, which is shorter than its diff:
```python
import jax
import jax.numpy as jnp
from jax import lax
from jax.experimental import pallas as pl
from jax.experimental.pallas import tpu as pltpu
from jax.sharding import PartitionSpec as P

CAP = 3
ITERS = 2
NZ = 8
NY = 4
NOV = 4
BATCH = 4
CHUNKS = 4
EARLY = 3
F32 = jnp.float32
BF16 = jnp.bfloat16
MESH = pl.DeviceIdType.MESH
Z_ORDER = (4, 3, 5, 2, 6, 1, 7)
NT = (((1,), (1,)), ((), ()))
PAIR, SELK, JSEL, RET, TAB = 0, 12, 24, 27, 43


def scan_pairs(pa_s, tab, z, y):
    def visit(p, carry):
        counts, found = carry
        counts, found = list(counts), list(found)
        for j in range(NY):
            atom = z * NY + ((y + j) & (NY - 1))
            hit = (pa_s[0, p] == atom) | (pa_s[1, p] == atom)
            for s in range(CAP):
                found[j * CAP + s] = jnp.where(hit & (counts[j] == s), p, found[j * CAP + s])
            counts[j] = counts[j] + hit.astype(jnp.int32)
        return tuple(counts), tuple(found)

    zero, none = jnp.int32(0), jnp.int32(-1)
    _, found = lax.fori_loop(0, NZ * NY, visit, ((zero,) * NY, (none,) * (NY * CAP)))
    for i in range(NY * CAP):
        pair = jnp.maximum(found[i], 0)
        tab[PAIR + i] = found[i]
        tab[SELK + i] = (z - (pair >> 2)) & (NZ - 1)
        if i < CAP:
            tab[JSEL + i] = (y - (pair & (NY - 1))) & (NY - 1)
    for k in range(NZ):
        pair = ((z + k) & (NZ - 1)) * NY + y
        for i in range(2):
            atom = pa_s[i, pair]
            j = (y - (atom & (NY - 1))) & (NY - 1)
            mate = ((NY - j) & (NY - 1)) * CAP
            rank = jnp.where(tab[PAIR + mate + 1] == pair, 1, 0) + jnp.where(
                tab[PAIR + mate + 2] == pair, 2, 0
            )
            tab[RET + 2 * k + i] = jnp.where((atom >> 2) == z, j * CAP + rank, -1)


def scratch(npno, npao, kaux):
    vm, dma, sm = pltpu.VMEM, pltpu.SemaphoreType.DMA, pltpu.SMEM
    rows = npno // CHUNKS
    square = (npno, npno)
    shapes = {
        "pa_s": sm((2, NZ * NY), jnp.int32),
        "pn_s": sm((1, NOV), jnp.int32),
        "sh_s": sm((1,), F32),
        "e_v": vm((1, npno), F32),
        "tab": sm((TAB,), jnp.int32),
        "f_v": vm((kaux, npao, npao), BF16),
        "s_v": vm((NOV,) + square, BF16),
        "i_v": vm(square, F32),
        "b_v": vm((npao, npno), BF16),
        "n_in": vm((NY - 1, 1, NOV), jnp.int32),
        "n_s": sm((NY - 1, 1, NOV), jnp.int32),
        "lhs_a": vm((CAP * EARLY * rows, npao), BF16),
        "lhs_b": vm((CAP * (CHUNKS - EARLY) * rows, npao), BF16),
        "b_t": vm((CAP, npno, npao), BF16),
        "half": vm((CAP, kaux * npno, npao), BF16),
        "g_v": vm((CAP, npno, kaux * npno), BF16),
        "p_v": vm((CAP, npno, kaux * npno), BF16),
        "cc": vm((CAP, 2 * npno, 2 * npno), BF16),
        "den": vm(square, F32),
        "base": vm(square, F32),
        "loc": dma((10,)),
        "nx": (dma((NY - 1,)), dma((NY - 1,))),
    }
    for c in range(CHUNKS):
        shapes[f"zb{c}"] = vm((NZ, rows, npao), BF16)
        shapes[f"ybo{c}"] = vm((NY - 1, CAP, rows, npao), BF16)
        shapes[f"yb{c}"] = vm((NY, CAP, rows, npao), BF16)
    shapes["zb"] = (dma((CHUNKS, NZ - 1)), dma((CHUNKS, NZ - 1)))
    shapes["yb"] = (dma((CHUNKS, NY - 1)), dma((CHUNKS, NY - 1)))
    for it in range(ITERS):
        shapes[f"zc{it}"] = vm((NZ,) + square, BF16)
        shapes[f"nc{it}"] = vm((2 * NZ,) + square, BF16)
        for s in range(CAP):
            shapes[f"yc{it}{s}"] = vm((NY,) + square, BF16)
        shapes[f"yco{it}"] = vm((CAP, NY - 1) + square, BF16)
        shapes[f"yn{it}"] = vm((NY, NOV) + square, BF16)
        shapes[f"yno{it}"] = vm((NY - 1, NOV) + square, BF16)
        shapes[f"yt{it}"] = vm((NY * CAP,) + square, BF16)
        shapes[f"bk{it}"] = vm((NZ,) + square, BF16)
        shapes[f"zt{it}"] = vm((NZ,) + square, BF16)
    shapes["zc"] = (dma((ITERS, NZ - 1)), dma((ITERS, NZ - 1)))
    shapes["yc"] = (dma((ITERS, CAP, NY - 1)), dma((ITERS, CAP, NY - 1)))
    shapes["fw"] = (dma((ITERS,)), dma((ITERS,)))
    shapes["yn"] = (dma((ITERS, NY - 1)), dma((ITERS, NY - 1)))
    shapes["yt"] = (dma((ITERS, CAP, NY - 1)), dma((ITERS, CAP, NY - 1)))
    shapes["zt"] = (dma((ITERS, NZ - 1)), dma((ITERS, NZ - 1)))
    flat = {}
    for name, shape in shapes.items():
        if isinstance(shape, tuple):
            flat[name + "_s"], flat[name + "_r"] = shape
        else:
            flat[name] = shape
    return flat


def kernel(names, pa_h, pn_h, sh_h, e_h, b_h, c_h, f_h, s_h, i_h, out, *refs):
    r = dict(zip(names, refs))
    tab, loc, half, g_v, p_v, cc = r["tab"], r["loc"], r["half"], r["g_v"], r["p_v"], r["cc"]
    g = lax.axis_index("grp")
    d = lax.axis_index("dev")
    z, y = d // NY, d % NY
    groups = lax.axis_size("grp")
    npno = c_h.shape[1]
    kaux = f_h.shape[0]
    rows = npno // CHUNKS

    def at_z(k):
        return {"grp": g, "dev": ((z + k) % NZ) * NY + y}

    def at_y(j):
        return {"grp": g, "dev": z * NY + (y + j) % NY}

    before = {"grp": (g + groups - 1) % groups, "dev": d}
    after = {"grp": (g + 1) % groups, "dev": d}

    sent = []

    def send(src, dst, name, index, where):
        copy = pltpu.make_async_remote_copy(
            src_ref=src, dst_ref=dst,
            send_sem=r[name + "_s"].at[index], recv_sem=r[name + "_r"].at[index],
            device_id=where, device_id_type=MESH,
        )
        copy.start()
        sent.append(copy)
        return copy

    def arrive(copies):
        for copy in copies:
            copy.wait_recv()

    def local(src, dst, number):
        copy = pltpu.make_async_copy(src, dst, loc.at[number])
        copy.start()
        return copy

    own_b = local(b_h, r["b_v"], 0)
    small = [
        local(pa_h, r["pa_s"], 1),
        local(pn_h, r["pn_s"], 2),
        local(sh_h, r["sh_s"], 3),
        local(e_h, r["e_v"], 4),
    ]
    own_c = local(c_h, r["zc0"].at[0], 5)
    own_f = local(f_h, r["f_v"], 6)
    own_s = local(s_h, r["s_v"], 7)
    own_i = local(i_h, r["i_v"], 8)

    barrier = pltpu.get_barrier_semaphore()
    partners = [at_z(k) for k in Z_ORDER] + [at_y(j) for j in range(1, NY)] + [before, after]
    for partner in partners:
        pl.semaphore_signal(barrier, inc=1, device_id=partner, device_id_type=MESH)
    cc[...] = jnp.zeros_like(cc)
    own_b.wait()
    flipped = r["b_v"][...].T
    for c in range(CHUNKS):
        r[f"zb{c}"][0] = flipped[c * rows:(c + 1) * rows]
    for copy in small:
        copy.wait()
    scan_pairs(r["pa_s"], tab, z, y)
    wide = jnp.broadcast_to(r["e_v"][...], (npno, npno))
    r["den"][...] = wide + wide.T + r["sh_s"][0]
    own_c.wait()
    pl.semaphore_wait(barrier, len(partners))

    zb = [
        [send(r[f"zb{c}"].at[0], r[f"zb{c}"].at[k], "zb", (c, k - 1), at_z(k)) for k in Z_ORDER]
        for c in range(CHUNKS)
    ]
    zc = [send(c_h, r["zc0"].at[k], "zc", (0, k - 1), at_z(k)) for k in Z_ORDER]
    nx = [send(pn_h, r["n_in"].at[j - 1], "nx", j - 1, at_y(j)) for j in range(1, NY)]

    yb = []
    for c in range(CHUNKS):
        arrive(zb[c])
        for j in range(1, NY):
            for s in range(CAP):
                r[f"ybo{c}"][j - 1, s] = r[f"zb{c}"][tab[SELK + j * CAP + s]]
            yb.append(
                send(r[f"ybo{c}"].at[j - 1], r[f"yb{c}"].at[j], "yb", (c, j - 1), at_y(j))
            )
        for s in range(CAP):
            r[f"yb{c}"][0, s] = r[f"zb{c}"][tab[SELK + s]]

    def collect(first, last, lhs):
        height = (last - first) * rows
        for s in range(CAP):
            for c in range(first, last):
                block = r[f"yb{c}"][tab[JSEL + s], s]
                lhs[pl.ds(s * height + (c - first) * rows, rows), :] = block
                r["b_t"][s, pl.ds(c * rows, rows), :] = block

    def first_product(first, last, lhs):
        height = (last - first) * rows

        def step(kk, carry):
            for u in range(BATCH):
                part = jnp.dot(
                    lhs[...], r["f_v"][kk * BATCH + u], preferred_element_type=F32
                ).astype(BF16)
                start = pl.multiple_of(kk * (npno * BATCH), npno * BATCH)
                for s in range(CAP):
                    half[s, pl.ds(start + u * npno + first * rows, height), :] = part[
                        s * height:(s + 1) * height
                    ]
            return carry

        lax.fori_loop(0, kaux // BATCH, step, 0)

    def share_amps(it, zc):
        arrive(zc)
        yc = []
        for s in range(CAP):
            for j in range(1, NY):
                r[f"yco{it}"][s, j - 1] = r[f"zc{it}"][tab[SELK + j * CAP + s]]
            yc.append([
                send(
                    r[f"yco{it}"].at[s, j - 1], r[f"yc{it}{s}"].at[j], "yc", (it, s, j - 1), at_y(j)
                )
                for j in range(1, NY)
            ])
            r[f"yc{it}{s}"][0] = r[f"zc{it}"][tab[SELK + s]]
        fw = send(r[f"zc{it}"], r[f"nc{it}"].at[pl.ds(NZ, NZ)], "fw", it, before)
        r[f"nc{it}"][:NZ] = r[f"zc{it}"][...]
        return yc, fw

    def place(listed):
        return (listed >> 5) * NZ + ((z - ((listed & 31) >> 2)) & (NZ - 1))

    def share_neighbours(it, fw):
        fw.wait_recv()
        yn = []
        for j in range(1, NY):
            for n in range(NOV):
                r[f"yno{it}"][j - 1, n] = r[f"nc{it}"][place(r["n_s"][NY - 1 - j, 0, n])]
            yn.append(
                send(r[f"yno{it}"].at[j - 1], r[f"yn{it}"].at[j], "yn", (it, j - 1), at_y(j))
            )
        for n in range(NOV):
            r[f"yn{it}"][0, n] = r[f"nc{it}"][place(r["pn_s"][0, n])]
        return yn

    arrive(nx)
    to_s = local(r["n_in"], r["n_s"], 9)
    own_f.wait()
    arrive(yb[:EARLY * (NY - 1)])
    collect(0, EARLY, r["lhs_a"])
    first_product(0, EARLY, r["lhs_a"])
    yc, fw = share_amps(0, zc)
    arrive(yb[EARLY * (NY - 1):])
    collect(EARLY, CHUNKS, r["lhs_b"])
    first_product(EARLY, CHUNKS, r["lhs_b"])

    def second_product(kk, carry):
        start = pl.multiple_of(kk * (npno * BATCH), npno * BATCH)
        for s in range(CAP):
            inner = lax.dot_general(
                half[s, pl.ds(start, npno * BATCH), :], r["b_t"][s], NT,
                preferred_element_type=F32,
            ).astype(BF16)
            for u in range(BATCH):
                g_v[s, :, pl.ds(start + u * npno, npno)] = inner[u * npno:(u + 1) * npno]
        return carry

    lax.fori_loop(0, kaux // BATCH, second_product, 0)
    to_s.wait()
    own_s.wait()
    own_i.wait()

    for it in range(ITERS):
        yt = []
        for s in range(CAP):
            arrive(yc[s])
            amps = r[f"yc{it}{s}"][tab[JSEL + s]]
            cc[s, :npno, :npno] = amps
            cc[s, npno:, npno:] = amps
            for h in range(kaux // 2):
                span = pl.ds(h * 2 * npno, 2 * npno)
                p_v[s, :, span] = jnp.dot(
                    g_v[s, :, span], cc[s], preferred_element_type=F32
                ).astype(BF16)
            term = lax.dot_general(p_v[s], g_v[s], NT, preferred_element_type=F32)
            r[f"yt{it}"][s] = term.astype(BF16)
            for j in range(1, NY):
                yt.append(
                    send(
                        r[f"yt{it}"].at[s], r[f"yt{it}"].at[j * CAP + s],
                        "yt", (it, s, j - 1), at_y(j),
                    )
                )
        yn = share_neighbours(it, fw)
        arrive(yt)
        zt = []
        for k in (0,) + Z_ORDER:
            total = jnp.zeros((npno, npno), F32)
            for i in range(2):
                slot = tab[RET + 2 * k + i]
                weight = (slot >= 0).astype(F32)
                total += r[f"yt{it}"][jnp.maximum(slot, 0)].astype(F32) * weight
            if k == 0:
                r["base"][...] = r["i_v"][...] + total
            else:
                r[f"bk{it}"][k] = total.astype(BF16)
                zt.append(
                    send(r[f"bk{it}"].at[k], r[f"zt{it}"].at[k], "zt", (it, k - 1), at_z(k))
                )
        arrive(yn)
        coupling = r["base"][...]
        for n in range(NOV):
            other = r[f"yn{it}"][(y - (r["pn_s"][0, n] & (NY - 1))) & (NY - 1), n]
            mixed = jnp.dot(r["s_v"][n], other, preferred_element_type=F32).astype(BF16)
            coupling += lax.dot_general(mixed, r["s_v"][n], NT, preferred_element_type=F32)
        r["base"][...] = coupling
        arrive(zt)
        total = r["base"][...]
        for k in range(1, NZ):
            total += r[f"zt{it}"][k].astype(F32)
        if it + 1 < ITERS:
            column = r[f"zc{it + 1}"]
            column[0] = (-total / r["den"][...]).astype(BF16)
            zc = [
                send(column.at[0], column.at[k], "zc", (it + 1, k - 1), at_z(k)) for k in Z_ORDER
            ]
            yc, fw = share_amps(it + 1, zc)
        else:
            out[...] = total
    for copy in sent:
        copy.wait_send()


def on_device(
    amplitudes,
    bases,
    factors,
    intersections,
    pair_integrals,
    pno_energies,
    pair_shift,
    pair_atoms,
    pair_next,
):
    npno, npao, kaux = amplitudes.shape[1], bases.shape[1], factors.shape[1]
    shapes = scratch(npno, npao, kaux)
    names = tuple(shapes)

    def body(*refs):
        kernel(names, *refs)

    total = pl.pallas_call(
        body,
        out_shape=jax.ShapeDtypeStruct((npno, npno), F32),
        in_specs=[pl.BlockSpec(memory_space=pl.ANY)] * 9,
        out_specs=pl.BlockSpec(memory_space=pltpu.VMEM),
        scratch_shapes=list(shapes.values()),
        compiler_params=pltpu.CompilerParams(
            collective_id=0, has_side_effects=True, vmem_limit_bytes=67043328
        ),
        name="ladder",
    )(
        pair_atoms.T, pair_next, pair_shift, pno_energies, bases[0], amplitudes[0], factors[0],
        intersections[0], pair_integrals[0],
    )
    denominator = pno_energies[0][:, None] + pno_energies[0][None, :] + pair_shift[0]
    return (-total / denominator)[None]


def solution(mesh):
    return jax.shard_map(
        on_device,
        mesh=mesh,
        in_specs=(
            P(("grp", "dev"), None, None),
            P(("grp", "dev"), None, None),
            P(("grp", "dev"), None, None, None),
            P(("grp", "dev"), None, None, None),
            P(("grp", "dev"), None, None),
            P(("grp", "dev"), None),
            P(("grp", "dev")),
            P("grp", None),
            P(("grp", "dev"), None),
        ),
        out_specs=P(("grp", "dev"), None, None),
        check_vma=False,
    )
```

time: 332 us -> 79.4 us (0.24)
  waiting for transfers between devices: 269 us -> 0 us
  Pallas kernels: 0 us -> 77 us
  matrix products: 23.4 us -> 0 us
  starting transfers between devices: 16.1 us -> 0 us
  between operations: 13.9 us -> 0.66 us
  local copies, waits for them, and re-layouts: 4.92 us -> 0 us
    all_gather x3 -> x0, waiting for transfers between devices: 229 us -> none  [the longest x2 154 us: on_device(): group_amps = lax.all_gather(current, 'dev', axis=0, tiled=True)]
    pallas_call x0 -> x1, Pallas kernels: none -> 77 us  [on_device(): pl.pallas_call(body, out_shape=jax.ShapeDtypeStruct((npno, npno), F32), i...]
    ppermute x2 -> x0, waiting for transfers between devices: 24.1 us -> none  [from_behind(): lax.ppermute(value, axis, [(source, source + steps) for source in range(f...]
    dot_general x12 -> x0, matrix products: 23.4 us -> none  [the longest x7 10.3 us: select_rows(): jnp.dot(selector, flat_rows, preferred_element_type=jnp.float32)]
    all_to_all x2 -> x0, waiting for transfers between devices: 13.9 us -> none  [on_device(): lax.all_to_all(spread, 'dev', split_axis=0, concat_axis=0, tiled=True)]
    all_to_all x2 -> x0, starting transfers between devices: 11.8 us -> none  [on_device(): lax.all_to_all(spread, 'dev', split_axis=0, concat_axis=0, tiled=True)]
    ppermute x2 -> x0, starting transfers between devices: 4.15 us -> none  [from_behind(): lax.ppermute(value, axis, [(source, source + steps) for source in range(f...]
  transfers between devices with their start and end apart: 7 -> 0, of which waited for: 7 -> 0; matrix products, arithmetic and copies ran while one was open for 2% -> 0% of each run, Pallas kernels for 0% -> 0%
where the time goes in v4:
time: 79.4 us; the launch traced here: 79.3 us
  Pallas kernels  77 us (97%)
  other arithmetic  1.58 us (2%)
    pallas_call x1, Pallas kernels, on_device(): pl.pallas_call(body, out_shape=jax.ShapeDtypeStruct((npno, npno), F32), i...  77 us

profile of v4, /device:TPU:4, one launch (start us, length us, event | category | flops | bytes accessed | tf_op | source)
XLA Modules:
  0.0 79.3 jit_solution(14977277372676993188)
XLA Ops:
  0.7 77.0 %ladder.1 = f32[128,128]{1,0:T(8,128)} custom-call(s32[2,32]{1,0:T(2,128)} %bitcast.17, s32[1,4]{1,0:T(1,128)} %refs_1_.1, f32[1]{0:T(128)} %copy.10.refs_2_, f32[1,128]{1,0:T(1,128)} %refs_3_.1, bf16[256,128]{1,0:T(8,128)(2,1)} %bitcast.13, bf16[128,128]{1,0:T(8,128)(2,1)} %bitcast.15, bf16[32,256,256]{2,1,0:T(8,128)(2,1)} %bitcast.11, ...), custom_call_target="tpu_custom_call" | custom-call | tf_op jit(solution)/shard_map/ladder/pallas_call | solution.py:369
  77.7 1.6 %divide_bitcast_fusion = f32[1,128,128]{2,1,0:T(8,128)} fusion(f32[128,128]{1,0:T(8,128)} %ladder.1, f32[]{:T(128)} %bitcast.10, f32[128]{0:T(128)} %bitcast.16), kind=kLoop, calls=%fused_computation | loop fusion | flops 65536 | bytes 131588 | tf_op jit(solution)/shard_map/broadcast_in_dim | solution.py:384

commit v5 on v4

--- a/solution.py
+++ b/solution.py
@@ -13,6 +13,7 @@
 BATCH = 4
 CHUNKS = 4
 EARLY = 3
+HALVES = 2
 F32 = jnp.float32
 BF16 = jnp.bfloat16
 MESH = pl.DeviceIdType.MESH
@@ -57,6 +58,7 @@
     vm, dma, sm = pltpu.VMEM, pltpu.SemaphoreType.DMA, pltpu.SMEM
     rows = npno // CHUNKS
     square = (npno, npno)
+    part = (npno // HALVES, npno)
     shapes = {
         "pa_s": sm((2, NZ * NY), jnp.int32),
         "pn_s": sm((1, NOV), jnp.int32),
@@ -78,7 +80,8 @@
         "cc": vm((CAP, 2 * npno, 2 * npno), BF16),
         "den": vm(square, F32),
         "base": vm(square, F32),
-        "loc": dma((10,)),
+        "mine": vm(square, F32),
+        "loc": dma((11,)),
         "nx": (dma((NY - 1,)), dma((NY - 1,))),
     }
     for c in range(CHUNKS):
@@ -88,22 +91,23 @@
     shapes["zb"] = (dma((CHUNKS, NZ - 1)), dma((CHUNKS, NZ - 1)))
     shapes["yb"] = (dma((CHUNKS, NY - 1)), dma((CHUNKS, NY - 1)))
     for it in range(ITERS):
-        shapes[f"zc{it}"] = vm((NZ,) + square, BF16)
-        shapes[f"nc{it}"] = vm((2 * NZ,) + square, BF16)
+        for h in range(HALVES):
+            shapes[f"zc{it}{h}"] = vm((NZ,) + part, BF16)
+            shapes[f"nc{it}{h}"] = vm((2 * NZ,) + part, BF16)
+            shapes[f"yt{it}{h}"] = vm((NY * CAP,) + part, BF16)
         for s in range(CAP):
-            shapes[f"yc{it}{s}"] = vm((NY,) + square, BF16)
-        shapes[f"yco{it}"] = vm((CAP, NY - 1) + square, BF16)
+            shapes[f"yc{it}{s}"] = vm((NY, HALVES) + part, BF16)
+        shapes[f"yco{it}"] = vm((HALVES, CAP, NY - 1) + part, BF16)
         shapes[f"yn{it}"] = vm((NY, NOV) + square, BF16)
         shapes[f"yno{it}"] = vm((NY - 1, NOV) + square, BF16)
-        shapes[f"yt{it}"] = vm((NY * CAP,) + square, BF16)
-        shapes[f"bk{it}"] = vm((NZ,) + square, BF16)
-        shapes[f"zt{it}"] = vm((NZ,) + square, BF16)
-    shapes["zc"] = (dma((ITERS, NZ - 1)), dma((ITERS, NZ - 1)))
-    shapes["yc"] = (dma((ITERS, CAP, NY - 1)), dma((ITERS, CAP, NY - 1)))
-    shapes["fw"] = (dma((ITERS,)), dma((ITERS,)))
+        shapes[f"bk{it}"] = vm((HALVES, NZ) + part, BF16)
+        shapes[f"zt{it}"] = vm((HALVES, NZ) + part, BF16)
+    shapes["zc"] = (dma((ITERS, HALVES, NZ - 1)), dma((ITERS, HALVES, NZ - 1)))
+    shapes["yc"] = (dma((ITERS, HALVES, CAP, NY - 1)), dma((ITERS, HALVES, CAP, NY - 1)))
+    shapes["fw"] = (dma((ITERS, HALVES)), dma((ITERS, HALVES)))
     shapes["yn"] = (dma((ITERS, NY - 1)), dma((ITERS, NY - 1)))
-    shapes["yt"] = (dma((ITERS, CAP, NY - 1)), dma((ITERS, CAP, NY - 1)))
-    shapes["zt"] = (dma((ITERS, NZ - 1)), dma((ITERS, NZ - 1)))
+    shapes["yt"] = (dma((ITERS, HALVES, CAP, NY - 1)), dma((ITERS, HALVES, CAP, NY - 1)))
+    shapes["zt"] = (dma((ITERS, HALVES, NZ - 1)), dma((ITERS, HALVES, NZ - 1)))
     flat = {}
     for name, shape in shapes.items():
         if isinstance(shape, tuple):
@@ -123,6 +127,8 @@
     npno = c_h.shape[1]
     kaux = f_h.shape[0]
     rows = npno // CHUNKS
+    part = npno // HALVES
+    span_of = [pl.ds(h * part, part) for h in range(HALVES)]
 
     def at_z(k):
         return {"grp": g, "dev": ((z + k) % NZ) * NY + y}
@@ -161,7 +167,7 @@
         local(sh_h, r["sh_s"], 3),
         local(e_h, r["e_v"], 4),
     ]
-    own_c = local(c_h, r["zc0"].at[0], 5)
+    own_c = [local(c_h.at[span_of[h]], r[f"zc0{h}"].at[0], (5, 10)[h]) for h in range(HALVES)]
     own_f = local(f_h, r["f_v"], 6)
     own_s = local(s_h, r["s_v"], 7)
     own_i = local(i_h, r["i_v"], 8)
@@ -180,14 +186,21 @@
     scan_pairs(r["pa_s"], tab, z, y)
     wide = jnp.broadcast_to(r["e_v"][...], (npno, npno))
     r["den"][...] = wide + wide.T + r["sh_s"][0]
-    own_c.wait()
+    for copy in own_c:
+        copy.wait()
     pl.semaphore_wait(barrier, len(partners))
 
     zb = [
         [send(r[f"zb{c}"].at[0], r[f"zb{c}"].at[k], "zb", (c, k - 1), at_z(k)) for k in Z_ORDER]
         for c in range(CHUNKS)
     ]
-    zc = [send(c_h, r["zc0"].at[k], "zc", (0, k - 1), at_z(k)) for k in Z_ORDER]
+    zc = [
+        [
+            send(c_h.at[span_of[h]], r[f"zc0{h}"].at[k], "zc", (0, h, k - 1), at_z(k))
+            for k in Z_ORDER
+        ]
+        for h in range(HALVES)
+    ]
     nx = [send(pn_h, r["n_in"].at[j - 1], "nx", j - 1, at_y(j)) for j in range(1, NY)]
 
     yb = []
@@ -228,36 +241,43 @@
         lax.fori_loop(0, kaux // BATCH, step, 0)
 
     def share_amps(it, zc):
-        arrive(zc)
-        yc = []
-        for s in range(CAP):
-            for j in range(1, NY):
-                r[f"yco{it}"][s, j - 1] = r[f"zc{it}"][tab[SELK + j * CAP + s]]
-            yc.append([
-                send(
-                    r[f"yco{it}"].at[s, j - 1], r[f"yc{it}{s}"].at[j], "yc", (it, s, j - 1), at_y(j)
-                )
-                for j in range(1, NY)
-            ])
-            r[f"yc{it}{s}"][0] = r[f"zc{it}"][tab[SELK + s]]
-        fw = send(r[f"zc{it}"], r[f"nc{it}"].at[pl.ds(NZ, NZ)], "fw", it, before)
-        r[f"nc{it}"][:NZ] = r[f"zc{it}"][...]
+        yc, fw = [[] for s in range(CAP)], []
+        for h in range(HALVES):
+            column, beside = r[f"zc{it}{h}"], r[f"nc{it}{h}"]
+            arrive(zc[h])
+            for s in range(CAP):
+                for j in range(1, NY):
+                    r[f"yco{it}"][h, s, j - 1] = column[tab[SELK + j * CAP + s]]
+                yc[s] += [
+                    send(
+                        r[f"yco{it}"].at[h, s, j - 1], r[f"yc{it}{s}"].at[j, h],
+                        "yc", (it, h, s, j - 1), at_y(j),
+                    )
+                    for j in range(1, NY)
+                ]
+                r[f"yc{it}{s}"][0, h] = column[tab[SELK + s]]
+            fw.append(send(column, beside.at[pl.ds(NZ, NZ)], "fw", (it, h), before))
+            beside[:NZ] = column[...]
         return yc, fw
 
     def place(listed):
         return (listed >> 5) * NZ + ((z - ((listed & 31) >> 2)) & (NZ - 1))
 
     def share_neighbours(it, fw):
-        fw.wait_recv()
+        arrive(fw)
         yn = []
         for j in range(1, NY):
             for n in range(NOV):
-                r[f"yno{it}"][j - 1, n] = r[f"nc{it}"][place(r["n_s"][NY - 1 - j, 0, n])]
+                index = place(r["n_s"][NY - 1 - j, 0, n])
+                for h in range(HALVES):
+                    r[f"yno{it}"][j - 1, n, span_of[h], :] = r[f"nc{it}{h}"][index]
             yn.append(
                 send(r[f"yno{it}"].at[j - 1], r[f"yn{it}"].at[j], "yn", (it, j - 1), at_y(j))
             )
         for n in range(NOV):
-            r[f"yn{it}"][0, n] = r[f"nc{it}"][place(r["pn_s"][0, n])]
+            index = place(r["pn_s"][0, n])
+            for h in range(HALVES):
+                r[f"yn{it}"][0, n, span_of[h], :] = r[f"nc{it}{h}"][index]
         return yn
 
     arrive(nx)
@@ -288,62 +308,80 @@
     own_i.wait()
 
     for it in range(ITERS):
-        yt = []
+        yt = [[] for h in range(HALVES)]
+
+        def send_term(s, h):
+            home = r[f"yt{it}{h}"]
+            for j in range(1, NY):
+                yt[h].append(
+                    send(home.at[s], home.at[j * CAP + s], "yt", (it, h, s, j - 1), at_y(j))
+                )
+
         for s in range(CAP):
             arrive(yc[s])
             amps = r[f"yc{it}{s}"][tab[JSEL + s]]
-            cc[s, :npno, :npno] = amps
-            cc[s, npno:, npno:] = amps
-            for h in range(kaux // 2):
-                span = pl.ds(h * 2 * npno, 2 * npno)
+            for h in range(HALVES):
+                cc[s, h * part:(h + 1) * part, :npno] = amps[h]
+                cc[s, npno + h * part:npno + (h + 1) * part, npno:] = amps[h]
+            for b in range(kaux // 2):
+                span = pl.ds(b * 2 * npno, 2 * npno)
                 p_v[s, :, span] = jnp.dot(
                     g_v[s, :, span], cc[s], preferred_element_type=F32
                 ).astype(BF16)
-            term = lax.dot_general(p_v[s], g_v[s], NT, preferred_element_type=F32)
-            r[f"yt{it}"][s] = term.astype(BF16)
-            for j in range(1, NY):
-                yt.append(
-                    send(
-                        r[f"yt{it}"].at[s], r[f"yt{it}"].at[j * CAP + s],
-                        "yt", (it, s, j - 1), at_y(j),
+            term = lax.dot_general(p_v[s], g_v[s], NT, preferred_element_type=F32).astype(BF16)
+            for h in range(HALVES):
+                r[f"yt{it}{h}"][s] = term[h * part:(h + 1) * part]
+            send_term(s, 0)
+            if s == 0:
+                send_term(s, 1)
+        for s in range(1, CAP):
+            send_term(s, 1)
+        yn = share_neighbours(it, fw)
+        zt = []
+        for h in range(HALVES):
+            arrive(yt[h])
+            copies = []
+            for k in Z_ORDER + (0,):
+                total = jnp.zeros((part, npno), F32)
+                for i in range(2):
+                    slot = tab[RET + 2 * k + i]
+                    weight = (slot >= 0).astype(F32)
+                    total += r[f"yt{it}{h}"][jnp.maximum(slot, 0)].astype(F32) * weight
+                if k == 0:
+                    r["mine"][span_of[h], :] = total
+                else:
+                    r[f"bk{it}"][h, k] = total.astype(BF16)
+                    copies.append(
+                        send(
+                            r[f"bk{it}"].at[h, k], r[f"zt{it}"].at[h, k],
+                            "zt", (it, h, k - 1), at_z(k),
+                        )
                     )
-                )
-        yn = share_neighbours(it, fw)
-        arrive(yt)
-        zt = []
-        for k in (0,) + Z_ORDER:
-            total = jnp.zeros((npno, npno), F32)
-            for i in range(2):
-                slot = tab[RET + 2 * k + i]
-                weight = (slot >= 0).astype(F32)
-                total += r[f"yt{it}"][jnp.maximum(slot, 0)].astype(F32) * weight
-            if k == 0:
-                r["base"][...] = r["i_v"][...] + total
-            else:
-                r[f"bk{it}"][k] = total.astype(BF16)
-                zt.append(
-                    send(r[f"bk{it}"].at[k], r[f"zt{it}"].at[k], "zt", (it, k - 1), at_z(k))
-                )
+            zt.append(copies)
         arrive(yn)
-        coupling = r["base"][...]
+        coupling = r["i_v"][...]
         for n in range(NOV):
             other = r[f"yn{it}"][(y - (r["pn_s"][0, n] & (NY - 1))) & (NY - 1), n]
             mixed = jnp.dot(r["s_v"][n], other, preferred_element_type=F32).astype(BF16)
             coupling += lax.dot_general(mixed, r["s_v"][n], NT, preferred_element_type=F32)
         r["base"][...] = coupling
-        arrive(zt)
-        total = r["base"][...]
-        for k in range(1, NZ):
-            total += r[f"zt{it}"][k].astype(F32)
+        zc = []
+        for h in range(HALVES):
+            arrive(zt[h])
+            total = r["base"][span_of[h], :] + r["mine"][span_of[h], :]
+            for k in range(1, NZ):
+                total += r[f"zt{it}"][h, k].astype(F32)
+            if it + 1 < ITERS:
+                column = r[f"zc{it + 1}{h}"]
+                column[0] = (-total / r["den"][span_of[h], :]).astype(BF16)
+                zc.append([
+                    send(column.at[0], column.at[k], "zc", (it + 1, h, k - 1), at_z(k))
+                    for k in Z_ORDER
+                ])
+            else:
+                out[span_of[h], :] = total
         if it + 1 < ITERS:
-            column = r[f"zc{it + 1}"]
-            column[0] = (-total / r["den"][...]).astype(BF16)
-            zc = [
-                send(column.at[0], column.at[k], "zc", (it + 1, k - 1), at_z(k)) for k in Z_ORDER
-            ]
             yc, fw = share_amps(it + 1, zc)
-        else:
-            out[...] = total
     for copy in sent:
         copy.wait_send()
 

time: 79.4 us -> 76.9 us (0.969)
  Pallas kernels: 77 us -> 74 us
    pallas_call x1, Pallas kernels: 77 us -> 74 us  [on_device(): pl.pallas_call(body, out_shape=jax.ShapeDtypeStruct((npno, npno), F32), i...]
where the time goes in v5:
time: 76.9 us; the launch traced here: 76.3 us
  Pallas kernels  74 us (96%)
  other arithmetic  1.58 us (2%)
    pallas_call x1, Pallas kernels, on_device(): pl.pallas_call(body, out_shape=jax.ShapeDtypeStruct((npno, npno), F32), i...  74 us
    broadcast_in_dim x1, other arithmetic, on_device(): return (-total / denominator)[None]  1.58 us

profile of v5, /device:TPU:4, one launch (start us, length us, event | category | flops | bytes accessed | tf_op | source)
XLA Modules:
  0.0 76.3 jit_solution(1193897201084107879)
XLA Ops:
  0.7 74.0 %ladder.1 = f32[128,128]{1,0:T(8,128)} custom-call(s32[2,32]{1,0:T(2,128)} %bitcast.17, s32[1,4]{1,0:T(1,128)} %refs_1_.1, f32[1]{0:T(128)} %copy.10.refs_2_, f32[1,128]{1,0:T(1,128)} %refs_3_.1, bf16[256,128]{1,0:T(8,128)(2,1)} %bitcast.13, bf16[128,128]{1,0:T(8,128)(2,1)} %bitcast.15, bf16[32,256,256]{2,1,0:T(8,128)(2,1)} %bitcast.11, ...), custom_call_target="tpu_custom_call" | custom-call | tf_op jit(solution)/shard_map/ladder/pallas_call | solution.py:407
  74.7 1.6 %divide_bitcast_fusion = f32[1,128,128]{2,1,0:T(8,128)} fusion(f32[128,128]{1,0:T(8,128)} %ladder.1, f32[]{:T(128)} %bitcast.10, f32[128]{0:T(128)} %bitcast.16), kind=kLoop, calls=%fused_computation | loop fusion | flops 65536 | bytes 131588 | tf_op jit(solution)/shard_map/broadcast_in_dim | solution.py:422

commit v6 on v5

--- a/solution.py
+++ b/solution.py
@@ -10,7 +10,7 @@
 NZ = 8
 NY = 4
 NOV = 4
-BATCH = 4
+BATCH = 8
 CHUNKS = 4
 EARLY = 3
 HALVES = 2
@@ -81,7 +81,7 @@
         "den": vm(square, F32),
         "base": vm(square, F32),
         "mine": vm(square, F32),
-        "loc": dma((11,)),
+        "loc": dma((13,)),
         "nx": (dma((NY - 1,)), dma((NY - 1,))),
     }
     for c in range(CHUNKS):
@@ -167,7 +167,7 @@
         local(sh_h, r["sh_s"], 3),
         local(e_h, r["e_v"], 4),
     ]
-    own_c = [local(c_h.at[span_of[h]], r[f"zc0{h}"].at[0], (5, 10)[h]) for h in range(HALVES)]
+    own_c = [local(c_h.at[span_of[h]], r[f"zc0{h}"].at[0], (5, 10, 11, 12)[h]) for h in range(HALVES)]
     own_f = local(f_h, r["f_v"], 6)
     own_s = local(s_h, r["s_v"], 7)
     own_i = local(i_h, r["i_v"], 8)
@@ -190,10 +190,41 @@
         copy.wait()
     pl.semaphore_wait(barrier, len(partners))
 
-    zb = [
-        [send(r[f"zb{c}"].at[0], r[f"zb{c}"].at[k], "zb", (c, k - 1), at_z(k)) for k in Z_ORDER]
-        for c in range(CHUNKS)
-    ]
+    zb = [{} for c in range(CHUNKS)]
+
+    def direct(c):
+        for k in (2, 6, 1, 7):
+            zb[c][k] = send(r[f"zb{c}"].at[0], r[f"zb{c}"].at[k], "zb", (c, k - 1), at_z(k))
+
+    def relay(c):
+        block = r[f"zb{c}"]
+        for held, hop, ahead in ((2, 1, 3), (6, 7, 5)):
+            zb[c][held].wait_recv()
+            if (held == 2) == (c % 2 == 0):
+                zb[c][4] = send(block.at[held], block.at[4], "zb", (c, 3), at_z(held))
+            zb[c][ahead] = send(block.at[held], block.at[ahead], "zb", (c, ahead - 1), at_z(hop))
+
+    yb = []
+
+    def cross(c):
+        arrive([zb[c][k] for k in (1, 7, 3, 5, 4)])
+        for j in range(1, NY):
+            for s in range(CAP):
+                r[f"ybo{c}"][j - 1, s] = r[f"zb{c}"][tab[SELK + j * CAP + s]]
+            yb.append(
+                send(r[f"ybo{c}"].at[j - 1], r[f"yb{c}"].at[j], "yb", (c, j - 1), at_y(j))
+            )
+        for s in range(CAP):
+            r[f"yb{c}"][0, s] = r[f"zb{c}"][tab[SELK + s]]
+
+    for c in range(CHUNKS - 1):
+        direct(c)
+    relay(0)
+    direct(CHUNKS - 1)
+    for c in range(1, CHUNKS - 1):
+        relay(c)
+    cross(0)
+    relay(CHUNKS - 1)
     zc = [
         [
             send(c_h.at[span_of[h]], r[f"zc0{h}"].at[k], "zc", (0, h, k - 1), at_z(k))
@@ -202,18 +233,8 @@
         for h in range(HALVES)
     ]
     nx = [send(pn_h, r["n_in"].at[j - 1], "nx", j - 1, at_y(j)) for j in range(1, NY)]
-
-    yb = []
-    for c in range(CHUNKS):
-        arrive(zb[c])
-        for j in range(1, NY):
-            for s in range(CAP):
-                r[f"ybo{c}"][j - 1, s] = r[f"zb{c}"][tab[SELK + j * CAP + s]]
-            yb.append(
-                send(r[f"ybo{c}"].at[j - 1], r[f"yb{c}"].at[j], "yb", (c, j - 1), at_y(j))
-            )
-        for s in range(CAP):
-            r[f"yb{c}"][0, s] = r[f"zb{c}"][tab[SELK + s]]
+    for c in range(1, CHUNKS):
+        cross(c)
 
     def collect(first, last, lhs):
         height = (last - first) * rows
@@ -240,25 +261,22 @@
 
         lax.fori_loop(0, kaux // BATCH, step, 0)
 
-    def share_amps(it, zc):
-        yc, fw = [[] for s in range(CAP)], []
-        for h in range(HALVES):
-            column, beside = r[f"zc{it}{h}"], r[f"nc{it}{h}"]
-            arrive(zc[h])
-            for s in range(CAP):
-                for j in range(1, NY):
-                    r[f"yco{it}"][h, s, j - 1] = column[tab[SELK + j * CAP + s]]
-                yc[s] += [
-                    send(
-                        r[f"yco{it}"].at[h, s, j - 1], r[f"yc{it}{s}"].at[j, h],
-                        "yc", (it, h, s, j - 1), at_y(j),
-                    )
-                    for j in range(1, NY)
-                ]
-                r[f"yc{it}{s}"][0, h] = column[tab[SELK + s]]
-            fw.append(send(column, beside.at[pl.ds(NZ, NZ)], "fw", (it, h), before))
-            beside[:NZ] = column[...]
-        return yc, fw
+    def share_half(it, h, copies, yc, fw):
+        column, beside = r[f"zc{it}{h}"], r[f"nc{it}{h}"]
+        arrive(copies)
+        for s in range(CAP):
+            for j in range(1, NY):
+                r[f"yco{it}"][h, s, j - 1] = column[tab[SELK + j * CAP + s]]
+            yc[s] += [
+                send(
+                    r[f"yco{it}"].at[h, s, j - 1], r[f"yc{it}{s}"].at[j, h],
+                    "yc", (it, h, s, j - 1), at_y(j),
+                )
+                for j in range(1, NY)
+            ]
+            r[f"yc{it}{s}"][0, h] = column[tab[SELK + s]]
+        fw.append(send(column, beside.at[pl.ds(NZ, NZ)], "fw", (it, h), before))
+        beside[:NZ] = column[...]
 
     def place(listed):
         return (listed >> 5) * NZ + ((z - ((listed & 31) >> 2)) & (NZ - 1))
@@ -285,8 +303,10 @@
     own_f.wait()
     arrive(yb[:EARLY * (NY - 1)])
     collect(0, EARLY, r["lhs_a"])
+    yc, fw = [[] for s in range(CAP)], []
     first_product(0, EARLY, r["lhs_a"])
-    yc, fw = share_amps(0, zc)
+    share_half(0, 0, zc[0], yc, fw)
+    share_half(0, 1, zc[1], yc, fw)
     arrive(yb[EARLY * (NY - 1):])
     collect(EARLY, CHUNKS, r["lhs_b"])
     first_product(EARLY, CHUNKS, r["lhs_b"])
@@ -331,11 +351,11 @@
             term = lax.dot_general(p_v[s], g_v[s], NT, preferred_element_type=F32).astype(BF16)
             for h in range(HALVES):
                 r[f"yt{it}{h}"][s] = term[h * part:(h + 1) * part]
-            send_term(s, 0)
-            if s == 0:
-                send_term(s, 1)
-        for s in range(1, CAP):
-            send_term(s, 1)
+            for h in range(HALVES if s == 0 else 1):
+                send_term(s, h)
+        for h in range(1, HALVES):
+            for s in range(1, CAP):
+                send_term(s, h)
         yn = share_neighbours(it, fw)
         zt = []
         for h in range(HALVES):
@@ -381,7 +401,9 @@
             else:
                 out[span_of[h], :] = total
         if it + 1 < ITERS:
-            yc, fw = share_amps(it + 1, zc)
+            yc, fw = [[] for s in range(CAP)], []
+            for h in range(HALVES):
+                share_half(it + 1, h, zc[h], yc, fw)
     for copy in sent:
         copy.wait_send()
 

time: 76.9 us -> 76 us (0.988)
  no operation moved by 1% of the time
where the time goes in v6:
time: 76 us; the launch traced here: 75.9 us
  Pallas kernels  73.7 us (97%)
  other arithmetic  1.58 us (2%)
    pallas_call x1, Pallas kernels, on_device(): pl.pallas_call(body, out_shape=jax.ShapeDtypeStruct((npno, npno), F32), i...  73.7 us
    broadcast_in_dim x1, other arithmetic, on_device(): return (-total / denominator)[None]  1.58 us

profile of v6, /device:TPU:4, one launch (start us, length us, event | category | flops | bytes accessed | tf_op | source)
XLA Modules:
  0.0 75.9 jit_solution(16698790618301688771)
XLA Ops:
  0.7 73.7 %ladder.1 = f32[128,128]{1,0:T(8,128)} custom-call(s32[2,32]{1,0:T(2,128)} %bitcast.17, s32[1,4]{1,0:T(1,128)} %refs_1_.1, f32[1]{0:T(128)} %copy.10.refs_2_, f32[1,128]{1,0:T(1,128)} %refs_3_.1, bf16[256,128]{1,0:T(8,128)(2,1)} %bitcast.13, bf16[128,128]{1,0:T(8,128)(2,1)} %bitcast.15, bf16[32,256,256]{2,1,0:T(8,128)(2,1)} %bitcast.11, ...), custom_call_target="tpu_custom_call" | custom-call | tf_op jit(solution)/shard_map/ladder/pallas_call | solution.py:429
  74.3 1.6 %divide_bitcast_fusion = f32[1,128,128]{2,1,0:T(8,128)} fusion(f32[128,128]{1,0:T(8,128)} %ladder.1, f32[]{:T(128)} %bitcast.10, f32[128]{0:T(128)} %bitcast.16), kind=kLoop, calls=%fused_computation | loop fusion | flops 65536 | bytes 131588 | tf_op jit(solution)/shard_map/broadcast_in_dim | solution.py:444

commit v7 on v6

--- a/solution.py
+++ b/solution.py
@@ -18,6 +18,7 @@
 BF16 = jnp.bfloat16
 MESH = pl.DeviceIdType.MESH
 Z_ORDER = (4, 3, 5, 2, 6, 1, 7)
+Y_ORDER = (1, 3, 2)
 NT = (((1,), (1,)), ((), ()))
 PAIR, SELK, JSEL, RET, TAB = 0, 12, 24, 27, 43
 
@@ -173,7 +174,7 @@
     own_i = local(i_h, r["i_v"], 8)
 
     barrier = pltpu.get_barrier_semaphore()
-    partners = [at_z(k) for k in Z_ORDER] + [at_y(j) for j in range(1, NY)] + [before, after]
+    partners = [at_z(k) for k in Z_ORDER] + [at_y(j) for j in Y_ORDER] + [before, after]
     for partner in partners:
         pl.semaphore_signal(barrier, inc=1, device_id=partner, device_id_type=MESH)
     cc[...] = jnp.zeros_like(cc)
@@ -208,7 +209,7 @@
 
     def cross(c):
         arrive([zb[c][k] for k in (1, 7, 3, 5, 4)])
-        for j in range(1, NY):
+        for j in Y_ORDER:
             for s in range(CAP):
                 r[f"ybo{c}"][j - 1, s] = r[f"zb{c}"][tab[SELK + j * CAP + s]]
             yb.append(
@@ -232,7 +233,7 @@
         ]
         for h in range(HALVES)
     ]
-    nx = [send(pn_h, r["n_in"].at[j - 1], "nx", j - 1, at_y(j)) for j in range(1, NY)]
+    nx = [send(pn_h, r["n_in"].at[j - 1], "nx", j - 1, at_y(j)) for j in Y_ORDER]
     for c in range(1, CHUNKS):
         cross(c)
 
@@ -265,14 +266,14 @@
         column, beside = r[f"zc{it}{h}"], r[f"nc{it}{h}"]
         arrive(copies)
         for s in range(CAP):
-            for j in range(1, NY):
+            for j in Y_ORDER:
                 r[f"yco{it}"][h, s, j - 1] = column[tab[SELK + j * CAP + s]]
             yc[s] += [
                 send(
                     r[f"yco{it}"].at[h, s, j - 1], r[f"yc{it}{s}"].at[j, h],
                     "yc", (it, h, s, j - 1), at_y(j),
                 )
-                for j in range(1, NY)
+                for j in Y_ORDER
             ]
             r[f"yc{it}{s}"][0, h] = column[tab[SELK + s]]
         fw.append(send(column, beside.at[pl.ds(NZ, NZ)], "fw", (it, h), before))
@@ -284,7 +285,7 @@
     def share_neighbours(it, fw):
         arrive(fw)
         yn = []
-        for j in range(1, NY):
+        for j in Y_ORDER:
             for n in range(NOV):
                 index = place(r["n_s"][NY - 1 - j, 0, n])
                 for h in range(HALVES):
@@ -332,7 +333,7 @@
 
         def send_term(s, h):
             home = r[f"yt{it}{h}"]
-            for j in range(1, NY):
+            for j in Y_ORDER:
                 yt[h].append(
                     send(home.at[s], home.at[j * CAP + s], "yt", (it, h, s, j - 1), at_y(j))
                 )

time: 76 us -> 75.3 us (level)
  Pallas kernels: 73.7 us -> 72.9 us
    pallas_call x1, Pallas kernels: 73.7 us -> 72.9 us  [on_device(): pl.pallas_call(body, out_shape=jax.ShapeDtypeStruct((npno, npno), F32), i...]
where the time goes in v7:
time: 75.3 us; the launch traced here: 75.1 us
  Pallas kernels  72.9 us (97%)
  other arithmetic  1.58 us (2%)
    pallas_call x1, Pallas kernels, on_device(): pl.pallas_call(body, out_shape=jax.ShapeDtypeStruct((npno, npno), F32), i...  72.9 us
    broadcast_in_dim x1, other arithmetic, on_device(): return (-total / denominator)[None]  1.58 us

profile of v7, /device:TPU:4, one launch (start us, length us, event | category | flops | bytes accessed | tf_op | source)
XLA Modules:
  0.0 75.1 jit_solution(1546791948841836902)
XLA Ops:
  0.7 72.9 %ladder.1 = f32[128,128]{1,0:T(8,128)} custom-call(s32[2,32]{1,0:T(2,128)} %bitcast.17, s32[1,4]{1,0:T(1,128)} %refs_1_.1, f32[1]{0:T(128)} %copy.10.refs_2_, f32[1,128]{1,0:T(1,128)} %refs_3_.1, bf16[256,128]{1,0:T(8,128)(2,1)} %bitcast.13, bf16[128,128]{1,0:T(8,128)(2,1)} %bitcast.15, bf16[32,256,256]{2,1,0:T(8,128)(2,1)} %bitcast.11, ...), custom_call_target="tpu_custom_call" | custom-call | tf_op jit(solution)/shard_map/ladder/pallas_call | solution.py:430
  73.5 1.6 %divide_bitcast_fusion = f32[1,128,128]{2,1,0:T(8,128)} fusion(f32[128,128]{1,0:T(8,128)} %ladder.1, f32[]{:T(128)} %bitcast.10, f32[128]{0:T(128)} %bitcast.16), kind=kLoop, calls=%fused_computation | loop fusion | flops 65536 | bytes 131588 | tf_op jit(solution)/shard_map/broadcast_in_dim | solution.py:445
